TPU v7x, 1024 devices: a whole 8x8x8 slice. The times are simulated.
1024 devices in a mesh: sx: 32 (over x, z_hi, core), sy: 32 (over y, z_lo).
Axes of the slice: x: 8, y: 8, z: 8 (z_hi: 2, z_lo: 4; z = z_hi * 4 + z_lo), core: 2. Of those that a mesh axis runs over, the one named last changes fastest.
Arguments:
- residual: float32 [1536, 1536, 128], P('sx', 'sy'), may hold values from -6 to 6
- labels: int32 [1536, 1536], P('sx', 'sy'), may hold values from 0 to 7
- region_kappa: float32 [8], replicated, may hold values from 1 to 16
- coarse_basis: float32 [8, 1536, 1536], P(None, 'sx', 'sy'), may hold values from -0.5 to 0.5
- primal_cells: int32 [32, 32, 8], P('sx', 'sy'), may hold values from 0 to 2303
- level_two: float32 [32, 256, 256], P('sx', 'sy'), may hold values from -12 to 12
- row_restrict: float32 [32, 256, 16], P('sx', 'sy'), may hold values from -0.375 to 0.375
- level_three: float32 [512, 512], P('sx'), may hold values from -12 to 12
- row_order: int32 [512], replicated, may hold values from 0 to 511, each once
Outputs:
- result: float32 [1536, 1536, 128], P('sx', 'sy')
Inputs may be any that keep to these rules, and one draw needn't show every extreme that they name: `primal_cells`: entry k of subdomain (i, j) is a cell index, row-major within that subdomain's 48 x 48 cells.
All inputs are finite; a program needn't handle non-finite values.
Results may differ from a plain program's by a relative error of at most 0.00012.
Values sent between devices are 32-bit elements; how exact they have to be, the bound alone decides.
No kernel may reach another device: no remote copies, remote signals or barrier semaphores. Data moves between devices by JAX's collectives and lax.ppermute only.
A program may use at most 32 MiB of HBM per device.

v0:
```python
import jax
import jax.numpy as jnp
from jax import lax
from jax.sharding import PartitionSpec as P

CHEB = 6


shift_mass = 1.0
lower_edge = 1.0
upper_edge = 144.0
highest = lax.Precision.HIGHEST


def extended(block, sides, width):
    for axis, dim in sides:
        count = lax.axis_size(axis)
        forward = [(i, i + 1) for i in range(count - 1)]
        backward = [(target, source) for source, target in forward]
        low = lax.ppermute(
            lax.slice_in_dim(block, block.shape[dim] - width, None, axis=dim), axis, forward
        )
        high = lax.ppermute(lax.slice_in_dim(block, 0, width, axis=dim), axis, backward)
        block = jnp.concatenate([low, block, high], axis=dim)
    return block


def stencil(padded, values_in):
    beside = padded[2:, 1:-1] + padded[:-2, 1:-1] + padded[1:-1, 2:] + padded[1:-1, :-2]
    return (4.0 + shift_mass) * values_in - beside


def chebyshev(rhs_field, apply_op):
    centre = 0.5 * (upper_edge + lower_edge)
    half_range = 0.5 * (upper_edge - lower_edge)
    sigma_ratio = centre / half_range
    rho_now = 1.0 / sigma_ratio
    direction = rhs_field / centre
    solution = direction
    remainder = rhs_field
    for sweep_index in range(CHEB):
        remainder = remainder - apply_op(direction)
        rho_next = 1.0 / (2.0 * sigma_ratio - rho_now)
        direction = rho_next * rho_now * direction + 2.0 * rho_next / half_range * remainder
        solution = solution + direction
        rho_now = rho_next
    return solution


def shards(
    residual,
    labels,
    region_kappa,
    coarse_basis,
    primal_cells,
    level_two,
    row_restrict,
    level_three,
    row_order,
):
    cells_x, cells_y, rhs_count = residual.shape
    coarse_count = coarse_basis.shape[0]
    onehot = (labels[..., None] == jnp.arange(region_kappa.shape[0], dtype=jnp.int32)).astype(
        jnp.float32
    )
    root_coef = jnp.sqrt(jnp.sum(onehot * region_kappa, axis=-1))[..., None]

    def apply_local(values_in):
        scaled_in = root_coef * values_in
        return root_coef * stencil(jnp.pad(scaled_in, ((1, 1), (1, 1), (0, 0))), scaled_in)

    z_first = chebyshev(residual, apply_local)
    scaled = root_coef * z_first
    padded = extended(scaled, (("sx", 0), ("sy", 1)), 1)
    slack_field = residual - root_coef * stencil(padded, scaled)
    cell_count = cells_x * cells_y
    slack_cells = slack_field.reshape(cell_count, rhs_count)
    basis_cells = coarse_basis.reshape(coarse_count, cell_count)
    picked = jnp.take(slack_cells, primal_cells.reshape(-1), axis=0)
    coarse_res = jnp.dot(basis_cells, slack_cells, precision=highest) + picked
    local_two = level_two[0]
    picked_cols = local_two
    coarse_two = jnp.dot(
        picked_cols, lax.all_gather(coarse_res, "sy", axis=0, tiled=True), precision=highest
    )
    local_restrict = row_restrict[0]
    partial_value = lax.dot_general(
        local_restrict, coarse_res, (((0,), (0,)), ((), ())), precision=highest
    )
    row_terms = lax.psum(partial_value, "sy")
    shard_piece = lax.all_gather(row_terms, "sx", axis=0, tiled=True)
    row_index = jnp.arange(shard_piece.shape[0], dtype=jnp.int32)
    placed_cols = jnp.take(row_order, row_index)
    picked_cols = jnp.take(level_three, placed_cols, axis=1)
    coarse_three = jnp.dot(picked_cols, shard_piece, precision=highest)
    coarse = coarse_two + jnp.dot(local_restrict, coarse_three, precision=highest)
    correction = lax.dot_general(basis_cells, coarse, (((0,), (0,)), ((), ())), precision=highest)
    return z_first + correction.reshape(cells_x, cells_y, rhs_count)


def solution(mesh):
    in_specs = (
        P("sx", "sy", None),
        P("sx", "sy"),
        P(),
        P(None, "sx", "sy"),
        P("sx", "sy", None),
        P("sx", "sy", None),
        P("sx", "sy", None),
        P("sx", None),
        P(),
    )
    out_specs = P("sx", "sy", None)
    return jax.shard_map(shards, mesh=mesh, in_specs=in_specs, out_specs=out_specs, check_vma=False)
```

profile of v0, /device:TPU:1, one launch (start us, length us, event | category | flops | bytes accessed | tf_op | source)
XLA Modules:
  0.0 259.8 jit_solution(2861794255765357268)
XLA Ops:
  0.0 0.9 select_reduce_fusion
  0.9 1.7 broadcast_multiply_fusion
  2.7 0.6 broadcast_multiply_fusion.5
  3.3 1.1 broadcast_multiply_fusion.4
  4.4 0.6 broadcast_multiply_fusion.3
  5.1 1.1 broadcast_multiply_fusion.2
  6.1 1.2 fusion.46
  7.4 2.5 broadcast_multiply_fusion.1
  9.9 16.1 %collective-permute-start = (f32[1,48,128]{2,1,0:T(8,128)S(1)}, f32[1,48,128]{2,1,0:T(8,128)S(1)}, u32[]{:S(2)}, u32[]{:S(2)}) collective-permute-start(f32[1,48,128]{2,1,0:T(8,128)S(1)} %get-tuple-element.21), channel_id=1, source_target_pairs={{32,0},{64,32},{96,64},{128,96},{160,128},{192,160},{224,192},{256... | collective-permute-start | bytes 73736 | tf_op jit(solution)/shard_map/ppermute | solution.py:23
  26.0 1.9 collective-permute-start.1
  28.0 0.6 compare_and_fusion.1
  28.6 3.5 %gather_fusion.1 = s32[512]{0:T(512)S(1)} fusion(s32[512]{0:T(512)S(1)} %copy-done.1, s32[1024]{0:T(1024)S(1)} %pad_clamp_fusion.1), kind=kCustom, calls=%fused_computation.1 | custom fusion | bytes 6144 | tf_op jit(solution)/shard_map/jit(_take)/gather | solution.py:93
  32.2 1.3 collective-permute-start.2
  33.5 4.9 %collective-permute-start.3 = (f32[50,1,128]{2,1,0:T(1,128)S(1)}, f32[50,1,128]{2,1,0:T(1,128)}, u32[]{:S(2)}, u32[]{:S(2)}) collective-permute-start(f32[50,1,128]{2,1,0:T(1,128)S(1)} %get-tuple-element.19), channel_id=1, source_target_pairs={{0,1},{1,2},{2,3},{3,4},{4,5},{5,6},{6,7},{7,8},{8,9},{9,10},{10,1... | collective-permute-start | bytes 76808 | tf_op jit(solution)/shard_map/ppermute | solution.py:20
  38.4 0.1 copy.20
  38.5 0.8 reshape.88
  39.3 1.6 gather_fusion.2
  40.9 0.6 copy-done.11
  41.5 2.5 fusion.42
  44.1 0.6 gather_fusion
  44.7 1.8 fusion.45
  46.4 65.3 %all_gather.6 = f32[256,128]{1,0:T(8,128)S(1)} all-gather(f32[8,128]{1,0:T(8,128)S(1)} %fusion.45), channel_id=1, replica_groups=mesh['sx'=32,'sy'=32] {'sy'}, dimensions={0}, use_global_device_ids=true | all-gather | bytes 135168 | tf_op jit(solution)/shard_map/all_gather | solution.py:84
  111.7 0.2 convolution_bitcast_fusion.1
  111.9 61.5 %psum.7 = f32[16,128]{1,0:T(8,128)S(1)} all-reduce(f32[16,128]{1,0:T(8,128)S(1)} %convolution_bitcast_fusion.1), channel_id=1, replica_groups=mesh['sx'=32,'sy'=32] {'sy'}, use_global_device_ids=true, to_apply=%region_1.2 | all-reduce | flops 2048 | bytes 16384 | tf_op jit(solution)/shard_map/psum | solution.py:90
  173.4 81.8 %all_gather.7 = f32[512,128]{1,0:T(8,128)S(1)} all-gather(f32[16,128]{1,0:T(8,128)S(1)} %psum.7), channel_id=1, replica_groups=mesh['sx'=32,'sy'=32] {'sx'}, dimensions={0}, use_global_device_ids=true | all-gather | bytes 270336 | tf_op jit(solution)/shard_map/all_gather | solution.py:91
  255.3 0.2 fusion.52
  255.4 0.7 fusion.47
  256.1 0.1 convolution_add_fusion
  256.2 1.1 convolution_bitcast_fusion
  257.4 0.4 copy.21
  257.8 0.9 copy-done.3
  258.7 1.1 add.204
  (40 shorter events, 0.2 us)
Async XLA Ops:
  0.0 255.3 %copy-start = (f32[1,8,256]{2,1,0:T(8,128)S(1)}, f32[1,8,256]{2,1,0:T(8,128)}, u32[]{:S(2)}) copy-start(f32[1,8,256]{2,1,0:T(8,128)} %param.14) | copy-start | bytes 24580
  0.9 6.5 %copy-start.4 = (f32[48,48]{1,0:T(8,128)}, f32[48,48]{1,0:T(8,128)S(1)}, u32[]{:S(2)}) copy-start(f32[48,48]{1,0:T(8,128)S(1)} %get-tuple-element.23) | copy-start | bytes 27652
  0.9 1.8 copy-start.2
  7.4 20.6 %copy-start.13 = (s32[1,1,8]{2,1,0:T(1,128)S(1)}, s32[1,1,8]{2,1,0:T(1,128)}, u32[]{:S(2)}) copy-start(s32[1,1,8]{2,1,0:T(1,128)} %param.13) | copy-start | bytes 100
  9.9 18.7 %copy-start.1 = (s32[512]{0:T(512)S(1)}, s32[512]{0:T(512)}, u32[]{:S(2)}) copy-start(s32[512]{0:T(512)} %param.17) | copy-start | bytes 6148
  9.9 22.3 %collective-permute-start = (f32[1,48,128]{2,1,0:T(8,128)S(1)}, f32[1,48,128]{2,1,0:T(8,128)S(1)}, u32[]{:S(2)}, u32[]{:S(2)}) collective-permute-start(f32[1,48,128]{2,1,0:T(8,128)S(1)} %get-tuple-element.21), channel_id=1, source_target_pairs={{32,0},{64,32},{96,64},{128,96},{160,128},{192,160},{224,192},{256... | collective-permute-start | bytes 73736 | tf_op jit(solution)/shard_map/ppermute | solution.py:23
  26.0 6.1 %collective-permute-start.1 = (f32[1,48,128]{2,1,0:T(8,128)S(1)}, f32[1,48,128]{2,1,0:T(8,128)S(1)}, u32[]{:S(2)}, u32[]{:S(2)}) collective-permute-start(f32[1,48,128]{2,1,0:T(8,128)S(1)} %get-tuple-element.20), channel_id=1, source_target_pairs={{0,32},{32,64},{64,96},{96,128},{128,160},{160,192},{192,224},{224... | collective-permute-start | bytes 73736 | tf_op jit(solution)/shard_map/ppermute | solution.py:20
  28.5 9.8 %copy-start.10 = (f32[16,512]{1,0:T(8,128)S(1)}, f32[16,512]{1,0:T(8,128)}, u32[]{:S(2)}) copy-start(f32[16,512]{1,0:T(8,128)} %param.16) | copy-start | bytes 98308
  32.1 6.5 %copy-start.5 = (f32[8,48,48]{2,1,0:T(8,128)S(1)}, f32[8,48,48]{2,1,0:T(8,128)}, u32[]{:S(2)}) copy-start(f32[8,48,48]{2,1,0:T(8,128)} %param.12) | copy-start | bytes 221188
  32.1 6.3 %copy-start.8 = (f32[1,48,128]{2,1,0:T(8,128)}, f32[1,48,128]{2,1,0:T(8,128)S(1)}, u32[]{:S(2)}) copy-start(f32[1,48,128]{2,1,0:T(8,128)S(1)} %collective-permute-done) | copy-start | bytes 73732
  32.1 6.2 %copy-start.9 = (f32[1,48,128]{2,1,0:T(8,128)}, f32[1,48,128]{2,1,0:T(8,128)S(1)}, u32[]{:S(2)}) copy-start(f32[1,48,128]{2,1,0:T(8,128)S(1)} %collective-permute-done.1) | copy-start | bytes 73732
  32.2 8.7 %collective-permute-start.2 = (f32[50,1,128]{2,1,0:T(1,128)S(1)}, f32[50,1,128]{2,1,0:T(1,128)S(1)}, u32[]{:S(2)}, u32[]{:S(2)}) collective-permute-start(f32[50,1,128]{2,1,0:T(1,128)S(1)} %get-tuple-element.18), channel_id=1, source_target_pairs={{1,0},{2,1},{3,2},{4,3},{5,4},{6,5},{7,6},{8,7},{9,8},{10,9},{11,1... | collective-permute-start | bytes 76808 | tf_op jit(solution)/shard_map/ppermute | solution.py:23
  33.5 8.0 %collective-permute-start.3 = (f32[50,1,128]{2,1,0:T(1,128)S(1)}, f32[50,1,128]{2,1,0:T(1,128)}, u32[]{:S(2)}, u32[]{:S(2)}) collective-permute-start(f32[50,1,128]{2,1,0:T(1,128)S(1)} %get-tuple-element.19), channel_id=1, source_target_pairs={{0,1},{1,2},{2,3},{3,4},{4,5},{5,6},{6,7},{7,8},{8,9},{9,10},{10,1... | collective-permute-start | bytes 76808 | tf_op jit(solution)/shard_map/ppermute | solution.py:20
  40.9 0.6 copy-start.11
  44.1 67.6 %copy-start.12 = (f32[1,8,16]{2,1,0:T(8,128)S(1)}, f32[1,8,16]{2,1,0:T(8,128)}, u32[]{:S(2)}) copy-start(f32[1,8,16]{2,1,0:T(8,128)} %param.15) | copy-start | bytes 1540
  44.1 211.4 %copy-start.6 = (f32[512,16]{1,0:T(8,128)S(1)}, f32[512,16]{1,0:T(8,128)}, u32[]{:S(2)}) copy-start(f32[512,16]{1,0:T(8,128)} %gather_fusion.2) | copy-start | bytes 98308
  44.7 211.6 %copy-start.7 = (f32[8,2304]{1,0:T(8,128)S(1)}, f32[8,2304]{1,0:T(8,128)}, u32[]{:S(2)}) copy-start(f32[8,2304]{1,0:T(8,128)} %reshape.88) | copy-start | bytes 221188
  257.4 1.3 copy-start.3
where the time goes:
time: 262 us; the launch traced here: 260 us
  blocking collectives  209 us (80%)
  starting transfers between devices  24.2 us (9%)
  other arithmetic  14.1 us (5%)
  local copies, waits for them, and re-layouts  8.48 us (3%)
  matrix products  4.08 us (2%)
    all_gather x1, blocking collectives, shards(): shard_piece = lax.all_gather(row_terms, 'sx', axis=0, tiled=True)  81.8 us
    all_gather x1, blocking collectives, shards(): lax.all_gather(coarse_res, 'sy', axis=0, tiled=True)  65.3 us
    psum x1, blocking collectives, shards(): row_terms = lax.psum(partial_value, 'sy')  61.5 us
    ppermute x2, starting transfers between devices, extended(): lax.ppermute(lax.slice_in_dim(block, 0, width, axis=dim), axis, backward)  17.4 us
    ppermute x2, starting transfers between devices, extended(): lax.ppermute(lax.slice_in_dim(block, block.shape[dim] - width, None, axis...  6.79 us
    mul x7, other arithmetic, apply_local(): scaled_in = root_coef * values_in  6.4 us
  transfers between devices with their start and end apart: 4, of which 0 were waited for; matrix products, arithmetic and copies ran while one was open for 3% of the time, Pallas kernels for 0%

commit v1 on v0

--- a/solution.py
+++ b/solution.py
@@ -12,17 +12,19 @@
 highest = lax.Precision.HIGHEST
 
 
-def extended(block, sides, width):
-    for axis, dim in sides:
-        count = lax.axis_size(axis)
-        forward = [(i, i + 1) for i in range(count - 1)]
-        backward = [(target, source) for source, target in forward]
-        low = lax.ppermute(
-            lax.slice_in_dim(block, block.shape[dim] - width, None, axis=dim), axis, forward
-        )
-        high = lax.ppermute(lax.slice_in_dim(block, 0, width, axis=dim), axis, backward)
-        block = jnp.concatenate([low, block, high], axis=dim)
-    return block
+def neighbour_edges(block, axis, dim):
+    count = lax.axis_size(axis)
+    forward = [(i, i + 1) for i in range(count - 1)]
+    backward = [(target, source) for source, target in forward]
+    low = lax.ppermute(lax.slice_in_dim(block, block.shape[dim] - 1, None, axis=dim), axis, forward)
+    high = lax.ppermute(lax.slice_in_dim(block, 0, 1, axis=dim), axis, backward)
+    return low, high
+
+
+def gathered(block, axis):
+    count = lax.axis_size(axis)
+    copies = jnp.broadcast_to(block[None], (count,) + block.shape)
+    return lax.all_to_all(copies, axis, 0, 0, tiled=True)
 
 
 def stencil(padded, values_in):
@@ -71,7 +73,12 @@
 
     z_first = chebyshev(residual, apply_local)
     scaled = root_coef * z_first
-    padded = extended(scaled, (("sx", 0), ("sy", 1)), 1)
+    row_low, row_high = neighbour_edges(scaled, "sx", 0)
+    col_low, col_high = neighbour_edges(scaled, "sy", 1)
+    tall = jnp.concatenate([row_low, scaled, row_high], axis=0)
+    padded = jnp.concatenate(
+        [jnp.pad(col_low, ((1, 1), (0, 0), (0, 0))), tall, jnp.pad(col_high, ((1, 1), (0, 0), (0, 0)))], axis=1
+    )
     slack_field = residual - root_coef * stencil(padded, scaled)
     cell_count = cells_x * cells_y
     slack_cells = slack_field.reshape(cell_count, rhs_count)
@@ -79,19 +86,19 @@
     picked = jnp.take(slack_cells, primal_cells.reshape(-1), axis=0)
     coarse_res = jnp.dot(basis_cells, slack_cells, precision=highest) + picked
     local_two = level_two[0]
-    picked_cols = local_two
-    coarse_two = jnp.dot(
-        picked_cols, lax.all_gather(coarse_res, "sy", axis=0, tiled=True), precision=highest
-    )
     local_restrict = row_restrict[0]
     partial_value = lax.dot_general(
         local_restrict, coarse_res, (((0,), (0,)), ((), ())), precision=highest
     )
-    row_terms = lax.psum(partial_value, "sy")
-    shard_piece = lax.all_gather(row_terms, "sx", axis=0, tiled=True)
-    row_index = jnp.arange(shard_piece.shape[0], dtype=jnp.int32)
-    placed_cols = jnp.take(row_order, row_index)
-    picked_cols = jnp.take(level_three, placed_cols, axis=1)
+    everyone = gathered(jnp.concatenate([coarse_res, partial_value], axis=0), "sy")
+    row_values = everyone[:, :coarse_count].reshape(-1, rhs_count)
+    row_terms = jnp.sum(everyone[:, coarse_count:], axis=0)
+    coarse_two = jnp.dot(local_two, row_values, precision=highest)
+    order_table = (
+        row_order[None, :] == jnp.arange(row_order.shape[0], dtype=jnp.int32)[:, None]
+    ).astype(jnp.float32)
+    picked_cols = jnp.dot(level_three, order_table, precision=highest)
+    shard_piece = gathered(row_terms, "sx").reshape(-1, rhs_count)
     coarse_three = jnp.dot(picked_cols, shard_piece, precision=highest)
     coarse = coarse_two + jnp.dot(local_restrict, coarse_three, precision=highest)
     correction = lax.dot_general(basis_cells, coarse, (((0,), (0,)), ((), ())), precision=highest)

time: 262 us -> 101 us (0.39)
  blocking collectives: 209 us -> 28.5 us
  waiting for transfers between devices: 0.01 us -> 15.4 us
  starting transfers between devices: 24.2 us -> 37.6 us
  local copies, waits for them, and re-layouts: 8.48 us -> 3.14 us
    all_gather x2 -> x0, blocking collectives: 147 us -> none  [the longest x1 81.8 us: shards(): shard_piece = lax.all_gather(row_terms, 'sx', axis=0, tiled=True)]
    psum x1 -> x0, blocking collectives: 61.5 us -> none  [shards(): row_terms = lax.psum(partial_value, 'sy')]
    all_to_all x0 -> x1, blocking collectives: none -> 28.5 us  [gathered(): return lax.all_to_all(copies, axis, 0, 0, tiled=True)]
    all_to_all x0 -> x1, waiting for transfers between devices: none -> 14.6 us  [gathered(): return lax.all_to_all(copies, axis, 0, 0, tiled=True)]
    all_to_all x0 -> x1, starting transfers between devices: none -> 14.1 us  [gathered(): return lax.all_to_all(copies, axis, 0, 0, tiled=True)]
    gather x2 -> x0, local copies, waits for them, and re-layouts: 5.13 us -> none  [the longest x1 3.49 us: shards(): placed_cols = jnp.take(row_order, row_index)]
  transfers between devices with their start and end apart: 4 -> 5, of which waited for: 0 -> 2; matrix products, arithmetic and copies ran while one was open for 3% -> 1% of each run, Pallas kernels for 0% -> 0%
where the time goes in v1:
time: 101 us
  starting transfers between devices  37.6 us (37%)
  blocking collectives  28.5 us (28%)
  waiting for transfers between devices  15.4 us (15%)
  other arithmetic  11.6 us (11%)
  matrix products  4.13 us (4%)
  local copies, waits for them, and re-layouts  3.14 us (3%)
    all_to_all x1, blocking collectives, gathered(): return lax.all_to_all(copies, axis, 0, 0, tiled=True)  28.5 us
    ppermute x2, starting transfers between devices, neighbour_edges(): high = lax.ppermute(lax.slice_in_dim(block, 0, 1, axis=dim), axis, backward)  17.3 us
    all_to_all x1, waiting for transfers between devices, gathered(): return lax.all_to_all(copies, axis, 0, 0, tiled=True)  14.6 us
    all_to_all x1, starting transfers between devices, gathered(): return lax.all_to_all(copies, axis, 0, 0, tiled=True)  14.1 us
    mul x7, other arithmetic, apply_local(): scaled_in = root_coef * values_in  6.28 us
    ppermute x2, starting transfers between devices, neighbour_edges(): lax.ppermute(lax.slice_in_dim(block, block.shape[dim] - 1, None, axis=dim...  6.19 us
    dot_general x1, matrix products, shards(): lax.dot_general(basis_cells, coarse, (((0,), (0,)), ((), ())), precision=...  2.16 us
  transfers between devices with their start and end apart: 5, of which 2 were waited for; matrix products, arithmetic and copies ran while one was open for 1% of the time, Pallas kernels for 0%

profile of v1, /device:TPU:1, one launch (start us, length us, event | category | flops | bytes accessed | tf_op | source)
XLA Modules:
  0.0 100.7 jit_solution(18201731300607266362)
XLA Ops:
  0.0 0.9 select_reduce_fusion
  0.9 0.0 copy-start.1
  0.9 1.7 %broadcast_multiply_fusion = f32[48,48,128]{2,1,0:T(8,128)S(1)} fusion(f32[48,48,128]{2,1,0:T(8,128)} %param.9, f32[48,48]{1,0:T(8,128)S(1)} %get-tuple-element.22), kind=kLoop, calls=%fused_computation.95 | loop fusion | flops 294912 | bytes 2368512 | tf_op jit(solution)/shard_map/mul | solution.py:71
  2.7 0.6 broadcast_multiply_fusion.5
  3.3 1.1 %broadcast_multiply_fusion.4 = (f32[48,48,128]{2,1,0:T(8,128)S(1)}, f32[48,48,128]{2,1,0:T(8,128)S(1)}, f32[48,48,128]{2,1,0:T(8,128)S(1)}) fusion(f32[48,48]{1,0:T(8,128)S(1)} %get-tuple-element.23, f32[48,48,128]{2,1,0:T(8,128)S(1)} %get-tuple-element.17, f32[48,48,128]{2,1,0:T(8,128)S(1)} %copy-done.1, f32[48,48,128]{2,1,0:T(8,128)S(1)} %get-tuple-element.16), kind=kLoop, calls=%fused_computation.99 | loop fusion | flops 4128768 | bytes 7087104 | tf_op jit(solution)/shard_map/mul | solution.py:71
  4.4 0.6 broadcast_multiply_fusion.3
  5.0 1.1 %broadcast_multiply_fusion.2 = (f32[48,48,128]{2,1,0:T(8,128)S(1)}, f32[48,48,128]{2,1,0:T(8,128)S(1)}) fusion(f32[48,48]{1,0:T(8,128)S(1)} %get-tuple-element.23, f32[48,48,128]{2,1,0:T(8,128)S(1)} %get-tuple-element.12, f32[48,48,128]{2,1,0:T(8,128)S(1)} %get-tuple-element.14, f32[48,48,128]{2,1,0:T(8,128)S(1)} %get-tuple-element.11), kind=kLoop, calls=%fused_computation.97 | loop fusion | flops 4128768 | bytes 5907456 | tf_op jit(solution)/shard_map/mul | solution.py:71
  6.1 1.2 %fusion.49 = (f32[48,48,128]{2,1,0:T(8,128)S(1)}, f32[48,48,128]{2,1,0:T(8,128)S(1)}) fusion(f32[48,48]{1,0:T(8,128)S(1)} %get-tuple-element.23, f32[48,48,128]{2,1,0:T(8,128)S(1)} %get-tuple-element.10, f32[48,48,128]{2,1,0:T(8,128)S(1)} %get-tuple-element.12, f32[48,48,128]{2,1,0:T(8,128)S(1)} %get-tuple-element.14, f32[48,48,128]{2,1,0:T(8,128)S(1)} %get-tuple-element.9), kind=kLoop, calls=%fused_computation.94 | loop fusion | flops 5013504 | bytes 7087104 | tf_op jit(solution)/shard_map/mul | solution.py:71
  7.3 0.0 copy-start.6
  7.3 1.7 %broadcast_multiply_fusion.1 = (f32[48,48,128]{2,1,0:T(8,128)S(1)}, f32[48,48,128]{2,1,0:T(8,128)S(1)}) fusion(f32[48,48]{1,0:T(8,128)S(1)} %get-tuple-element.23, f32[48,48,128]{2,1,0:T(8,128)S(1)} %get-tuple-element.8, f32[48,48,128]{2,1,0:T(8,128)S(1)} %get-tuple-element.7, f32[48,48,128]{2,1,0:T(8,128)S(1)} %get-tuple-element.10, ...), kind=kLoop, calls=%fused_computation.96 | loop fusion | flops 8847360 | bytes 10626048 | tf_op jit(solution)/shard_map/mul | solution.py:75
  9.0 16.0 %collective-permute-start = (f32[1,48,128]{2,1,0:T(8,128)S(1)}, f32[1,48,128]{2,1,0:T(8,128)S(1)}, u32[]{:S(2)}, u32[]{:S(2)}) collective-permute-start(f32[1,48,128]{2,1,0:T(8,128)S(1)} %get-tuple-element.21), channel_id=1, source_target_pairs={{32,0},{64,32},{96,64},{128,96},{160,128},{192,160},{224,192},{256... | collective-permute-start | bytes 73736 | tf_op jit(solution)/shard_map/ppermute | solution.py:20
  25.0 1.9 %collective-permute-start.1 = (f32[1,48,128]{2,1,0:T(8,128)S(1)}, f32[1,48,128]{2,1,0:T(8,128)S(1)}, u32[]{:S(2)}, u32[]{:S(2)}) collective-permute-start(f32[1,48,128]{2,1,0:T(8,128)S(1)} %get-tuple-element.20), channel_id=1, source_target_pairs={{0,32},{32,64},{64,96},{96,128},{128,160},{160,192},{192,224},{224... | collective-permute-start | bytes 73736 | tf_op jit(solution)/shard_map/ppermute | solution.py:19
  27.0 1.3 %collective-permute-start.2 = (f32[48,1,128]{2,1,0:T(1,128)S(1)}, f32[48,1,128]{2,1,0:T(1,128)S(1)}, u32[]{:S(2)}, u32[]{:S(2)}) collective-permute-start(f32[48,1,128]{2,1,0:T(1,128)S(1)} %get-tuple-element.18), channel_id=1, source_target_pairs={{1,0},{2,1},{3,2},{4,3},{5,4},{6,5},{7,6},{8,7},{9,8},{10,9},{11,1... | collective-permute-start | bytes 73736 | tf_op jit(solution)/shard_map/ppermute | solution.py:20
  28.3 4.3 %collective-permute-start.3 = (f32[48,1,128]{2,1,0:T(1,128)S(1)}, f32[48,1,128]{2,1,0:T(1,128)S(1)}, u32[]{:S(2)}, u32[]{:S(2)}) collective-permute-start(f32[48,1,128]{2,1,0:T(1,128)S(1)} %get-tuple-element.19), channel_id=1, source_target_pairs={{0,1},{1,2},{2,3},{3,4},{4,5},{5,6},{6,7},{7,8},{8,9},{9,10},{10,1... | collective-permute-start | bytes 73736 | tf_op jit(solution)/shard_map/ppermute | solution.py:19
  32.6 0.8 collective-permute-done.3
  33.5 1.5 %fusion.43 = f32[48,48,128]{2,1,0:T(8,128)S(1)} fusion(f32[48,48,128]{2,1,0:T(8,128)S(1)} %copy-done.1, f32[48,1,128]{2,1,0:T(1,128)S(1)} %collective-permute-done.3, f32[1,48,128]{2,1,0:T(8,128)S(1)} %collective-permute-done, f32[48,48,128]{2,1,0:T(8,128)S(1)} %get-tuple-element.5, f32[1,48,128]{2,1,0:T(8,128)S(1)} %collective-permute-done.1, ...), kind=kLoop, calls=%fused_computation.70 | loop fusion | flops 6193152 | bytes 3646464 | tf_op jit(solution)/shard_map/sub | solution.py:82
  35.0 0.6 gather_fusion
  35.6 0.8 fusion.47
  36.4 0.2 convolution_bitcast_fusion.1
  36.6 0.0 copy-start.3
  36.6 28.5 %all_to_all.10 = f32[32,24,128]{2,1,0:T(8,128)S(1)} all-to-all(f32[32,24,128]{2,1,0:T(8,128)S(1)} %broadcast_in_dim.16), channel_id=1, replica_groups=mesh['sx'=32,'sy'=32] {'sy'}, dimensions={0} | all-to-all | bytes 786432 | tf_op jit(solution)/shard_map/all_to_all | solution.py:27
  65.2 0.7 broadcast_in_dim.17
  65.9 14.1 %all-to-all-start.1 = ((f32[32,16,128]{2,1,0:T(8,128)}), f32[32,16,128]{2,1,0:T(8,128)S(1)}, u32[]{:S(2)}, u32[]{:S(2)}) async-start(f32[32,16,128]{2,1,0:T(8,128)} %broadcast_in_dim.17), calls=%async_computation.1 | async-start | bytes 524288 | tf_op jit(solution)/shard_map/all_to_all | solution.py:27
  80.1 0.1 reshape.67
  80.2 0.4 fusion.48
  80.6 0.2 fusion.52
  80.8 14.6 %all-to-all-done.1 = f32[32,16,128]{2,1,0:T(8,128)S(1)} async-done(((f32[32,16,128]{2,1,0:T(8,128)}), f32[32,16,128]{2,1,0:T(8,128)S(1)}, u32[]{:S(2)}, u32[]{:S(2)}) %all-to-all-start.1) | async-done | bytes 262176 | tf_op jit(solution)/shard_map/all_to_all | solution.py:27
  95.4 0.2 fusion.65
  95.7 0.1 convolution_add_fusion
  95.8 2.2 %convolution_bitcast_fusion = f32[2304,128]{0,1:T(8,128)} fusion(f32[128,8]{0,1:T(8,128)S(1)} %convolution_add_fusion, f32[8,2304]{1,0:T(8,128)S(1)} %reshape.67), kind=kOutput, calls=%fused_computation.1 | convolution fusion | flops 28311552 | bytes 1257472 | tf_op jit(solution)/shard_map/dot_general | solution.py:104
  98.0 1.6 %copy.15 = f32[2304,128]{1,0:T(8,128)S(1)} copy(f32[2304,128]{0,1:T(8,128)} %convolution_bitcast_fusion) | data formatting | bytes 2359296 | tf_op jit(solution)/shard_map/dot_general | solution.py:104
  99.6 1.2 %add.177 = f32[48,48,128]{2,1,0:T(8,128)} add(f32[48,48,128]{2,1,0:T(8,128)S(1)} %get-tuple-element.6, f32[48,48,128]{2,1,0:T(8,128)S(1)} %bitcast.39) | non-fusion elementwise | flops 294912 | bytes 3538944 | tf_op jit(solution)/shard_map/add | solution.py:105
  (23 shorter events, 0.2 us)
Async XLA Ops:
  0.0 80.2 %copy-start = (f32[16,512]{1,0:T(8,128)S(1)}, f32[16,512]{1,0:T(8,128)}, u32[]{:S(2)}) copy-start(f32[16,512]{1,0:T(8,128)} %param.16) | copy-start | bytes 98308
  0.9 1.8 %copy-start.1 = (f32[48,48,128]{2,1,0:T(8,128)S(1)}, f32[48,48,128]{2,1,0:T(8,128)}, u32[]{:S(2)}) copy-start(f32[48,48,128]{2,1,0:T(8,128)} %param.9) | copy-start | bytes 3538948
  7.3 25.3 %copy-start.6 = (s32[1,1,8]{2,1,0:T(1,128)S(1)}, s32[1,1,8]{2,1,0:T(1,128)}, u32[]{:S(2)}) copy-start(s32[1,1,8]{2,1,0:T(1,128)} %param.13) | copy-start | bytes 100
  9.0 23.6 %collective-permute-start = (f32[1,48,128]{2,1,0:T(8,128)S(1)}, f32[1,48,128]{2,1,0:T(8,128)S(1)}, u32[]{:S(2)}, u32[]{:S(2)}) collective-permute-start(f32[1,48,128]{2,1,0:T(8,128)S(1)} %get-tuple-element.21), channel_id=1, source_target_pairs={{32,0},{64,32},{96,64},{128,96},{160,128},{192,160},{224,192},{256... | collective-permute-start | bytes 73736 | tf_op jit(solution)/shard_map/ppermute | solution.py:20
  25.0 7.6 %collective-permute-start.1 = (f32[1,48,128]{2,1,0:T(8,128)S(1)}, f32[1,48,128]{2,1,0:T(8,128)S(1)}, u32[]{:S(2)}, u32[]{:S(2)}) collective-permute-start(f32[1,48,128]{2,1,0:T(8,128)S(1)} %get-tuple-element.20), channel_id=1, source_target_pairs={{0,32},{32,64},{64,96},{96,128},{128,160},{160,192},{192,224},{224... | collective-permute-start | bytes 73736 | tf_op jit(solution)/shard_map/ppermute | solution.py:19
  27.0 5.7 %collective-permute-start.2 = (f32[48,1,128]{2,1,0:T(1,128)S(1)}, f32[48,1,128]{2,1,0:T(1,128)S(1)}, u32[]{:S(2)}, u32[]{:S(2)}) collective-permute-start(f32[48,1,128]{2,1,0:T(1,128)S(1)} %get-tuple-element.18), channel_id=1, source_target_pairs={{1,0},{2,1},{3,2},{4,3},{5,4},{6,5},{7,6},{8,7},{9,8},{10,9},{11,1... | collective-permute-start | bytes 73736 | tf_op jit(solution)/shard_map/ppermute | solution.py:20
  28.3 5.2 %collective-permute-start.3 = (f32[48,1,128]{2,1,0:T(1,128)S(1)}, f32[48,1,128]{2,1,0:T(1,128)S(1)}, u32[]{:S(2)}, u32[]{:S(2)}) collective-permute-start(f32[48,1,128]{2,1,0:T(1,128)S(1)} %get-tuple-element.19), channel_id=1, source_target_pairs={{0,1},{1,2},{2,3},{3,4},{4,5},{5,6},{6,7},{7,8},{8,9},{9,10},{10,1... | collective-permute-start | bytes 73736 | tf_op jit(solution)/shard_map/ppermute | solution.py:19
  32.6 3.0 %copy-start.2 = (f32[8,48,48]{2,1,0:T(8,128)S(1)}, f32[8,48,48]{2,1,0:T(8,128)}, u32[]{:S(2)}) copy-start(f32[8,48,48]{2,1,0:T(8,128)} %param.12) | copy-start | bytes 221188
  35.0 1.4 %copy-start.4 = (f32[1,8,16]{2,1,0:T(8,128)S(1)}, f32[1,8,16]{2,1,0:T(8,128)}, u32[]{:S(2)}) copy-start(f32[1,8,16]{2,1,0:T(8,128)} %param.15) | copy-start | bytes 1540
  36.6 43.6 %copy-start.5 = (s32[512]{0:T(512)S(1)}, s32[512]{0:T(512)}, u32[]{:S(2)}) copy-start(s32[512]{0:T(512)} %param.17) | copy-start | bytes 6148
  36.6 44.0 %copy-start.3 = (f32[1,8,256]{2,1,0:T(8,128)S(1)}, f32[1,8,256]{2,1,0:T(8,128)}, u32[]{:S(2)}) copy-start(f32[1,8,256]{2,1,0:T(8,128)} %param.14) | copy-start | bytes 24580
  65.9 29.5 %all-to-all-start.1 = ((f32[32,16,128]{2,1,0:T(8,128)}), f32[32,16,128]{2,1,0:T(8,128)S(1)}, u32[]{:S(2)}, u32[]{:S(2)}) async-start(f32[32,16,128]{2,1,0:T(8,128)} %broadcast_in_dim.17), calls=%async_computation.1 | async-start | bytes 524288 | tf_op jit(solution)/shard_map/all_to_all | solution.py:27

commit v2 on v1

v2 whole, which is shorter than its diff:
```python
import jax
import jax.numpy as jnp
from jax import lax
from jax.experimental import pallas as pl
from jax.experimental.pallas import tpu as pltpu
from jax.sharding import PartitionSpec as P

CHEB = 6


shift_mass = 1.0
lower_edge = 1.0
upper_edge = 144.0
highest = lax.Precision.HIGHEST
f32 = jnp.float32
VMEM_LIMIT = 20 * 1024 * 1024


def sweep_factors():
    centre = 0.5 * (upper_edge + lower_edge)
    half_range = 0.5 * (upper_edge - lower_edge)
    sigma_ratio = centre / half_range
    rho_now = 1.0 / sigma_ratio
    factors = []
    for sweep_index in range(CHEB):
        rho_next = 1.0 / (2.0 * sigma_ratio - rho_now)
        factors.append((rho_next * rho_now, 2.0 * rho_next / half_range))
        rho_now = rho_next
    return 1.0 / centre, factors


def dot(a, b, dims=((1,), (0,))):
    return lax.dot_general(a, b, (dims, ((), ())), precision=highest, preferred_element_type=f32)


def solve_kernel(
    kappa,
    labels,
    residual,
    first,
    slack,
    row_first,
    row_last,
    col_first,
    col_last,
    root_out,
    zs,
    wide,
    rhs,
    coef,
):
    n, m = labels.shape
    here = labels[...]
    kap = jnp.full(here.shape, kappa[0], f32)
    for region in range(1, kappa.shape[0]):
        kap = jnp.where(here == region, kappa[region], kap)
    root_out[...] = jnp.sqrt(kap)
    kap_t = kap.T
    scale, factors = sweep_factors()
    lanes = residual.shape[2]
    zero_row = jnp.zeros((8, lanes), f32)
    for buffer in (rhs, zs):
        buffer[0] = jnp.zeros(zs.shape[1:], f32)
        buffer[n + 1] = jnp.zeros(zs.shape[1:], f32)
        for i in range(1, n + 1):
            buffer[i, 0:8] = zero_row
            buffer[i, 8 + m :] = zero_row

    for i in range(n):
        spread = jnp.broadcast_to(kap_t[:, i : i + 1], (m, lanes))
        coef[i] = spread
        rhs[i + 1, 8 : 8 + m] = (spread * lax.rsqrt(spread)) * residual[i]

    def neighbours(source, i, before, here_row):
        after = source[i + 2, 8 : 8 + m]
        beside = (before + after) + (source[i + 1, 7 : 7 + m] + source[i + 1, 9 : 9 + m])
        return after, coef[i] * (beside - (4.0 + shift_mass) * here_row)

    unroll = 4
    for sweep, (keep, add) in enumerate(factors):

        def some_rows(block, carry, sweep=sweep, keep=keep, add=add):
            before, here_row = carry
            for step in range(unroll):
                i = block * unroll + step
                if sweep == 0:
                    after, product = neighbours(rhs, i, before, here_row)
                    moved = (keep * scale + add) * here_row + (add * scale) * product
                    zs[i + 1, 8 : 8 + m] = scale * here_row + moved
                else:
                    after, product = neighbours(zs, i, before, here_row)
                    moved = keep * wide[i] + add * (rhs[i + 1, 8 : 8 + m] + product)
                    zs[i + 1, 8 : 8 + m] = here_row + moved
                wide[i] = moved
                before, here_row = here_row, after
            return before, here_row

        source = rhs if sweep == 0 else zs
        lax.fori_loop(0, n // unroll, some_rows, (jnp.zeros((m, lanes), f32), source[1, 8 : 8 + m]))

    before, here_row = jnp.zeros((m, lanes), f32), zs[1, 8 : 8 + m]
    row_first[...] = here_row
    row_last[...] = zs[n, 8 : 8 + m]
    for i in range(n):
        after, product = neighbours(zs, i, before, here_row)
        inv = lax.rsqrt(coef[i])
        slack[i] = (rhs[i + 1, 8 : 8 + m] + product) * inv
        first[i] = here_row * inv
        col_first[i : i + 1] = here_row[0:1]
        col_last[i : i + 1] = here_row[m - 1 : m]
        before, here_row = here_row, after


def solve(residual, labels, region_kappa):
    n, m, lanes = residual.shape
    field = jax.ShapeDtypeStruct((n, m, lanes), f32)
    edge_x = jax.ShapeDtypeStruct((m, lanes), f32)
    edge_y = jax.ShapeDtypeStruct((n, lanes), f32)
    whole = pl.BlockSpec(memory_space=pltpu.VMEM)
    return pl.pallas_call(
        solve_kernel,
        out_shape=(field, field, edge_x, edge_x, edge_y, edge_y, jax.ShapeDtypeStruct((n, m), f32)),
        in_specs=[
            pl.BlockSpec(memory_space=pltpu.SMEM),
            whole,
            whole,
        ],
        out_specs=[whole] * 7,
        scratch_shapes=[
            pltpu.VMEM((n + 2, m + 16, lanes), f32),
            pltpu.VMEM((n, m, lanes), f32),
            pltpu.VMEM((n + 2, m + 16, lanes), f32),
            pltpu.VMEM((n, m, lanes), f32),
        ],
        compiler_params=pltpu.CompilerParams(vmem_limit_bytes=VMEM_LIMIT),
        cost_estimate=pl.CostEstimate(
            flops=80 * n * m * lanes, bytes_accessed=12 * n * m * lanes, transcendentals=0
        ),
        name="solve",
    )(region_kappa, labels, residual)


def chosen_cells(primal, width):
    function = lax.broadcasted_iota(jnp.int32, (primal.shape[0], width), 0)
    cells = jnp.full(function.shape, primal[0], jnp.int32)
    for k in range(1, primal.shape[0]):
        cells = jnp.where(function == k, primal[k], cells)
    return cells


def inner_kernel(primal, basis, slack, out):
    cell = lax.broadcasted_iota(jnp.int32, basis.shape, 1)
    weights = basis[...] + jnp.where(cell == chosen_cells(primal, basis.shape[1]), 1.0, 0.0)
    out[...] = dot(weights, slack[...])


def restrict_kernel(
    primal,
    partial,
    basis,
    basis_first,
    basis_last,
    root,
    row_low,
    row_high,
    col_low,
    col_high,
    restrict,
    permuted,
    out,
):
    n, m = root.shape
    here = root[...]
    turned = here.T
    last = (n - 1) * m

    def share(weights, begin, stride, scale, halo):
        cell = begin + stride * lax.broadcasted_iota(jnp.int32, weights.shape, 1)
        weights = weights + jnp.where(cell == chosen_cells(primal, weights.shape[1]), 1.0, 0.0)
        return dot(weights * scale, halo[...])

    coarse_res = (
        partial[...]
        + (share(basis[:, 0:m], 0, 1, here[0:1], row_low) + share(basis[:, last:], last, 1, here[n - 1 :], row_high))
        + (
            share(basis_first[...], 0, m, turned[0:1], col_low)
            + share(basis_last[...], m - 1, m, turned[m - 1 :], col_high)
        )
    )
    terms = dot(restrict[...], coarse_res, ((0,), (0,)))
    both = jnp.concatenate([coarse_res, terms], axis=0)
    for member in range(out.shape[0]):
        out[member] = both


def row_kernel(everyone, local_two, two, out):
    members, height, lanes = everyone.shape
    count = two.shape[0]
    values = jnp.concatenate([everyone[member, 0:count] for member in range(members)], axis=0)
    two[...] = dot(local_two[...], values)
    terms = everyone[0, count:]
    for member in range(1, members):
        terms = terms + everyone[member, count:]
    for member in range(out.shape[0]):
        out[member] = terms


def split(values):
    high = values.astype(jnp.bfloat16).astype(f32)
    rest = values - high
    mid = rest.astype(jnp.bfloat16).astype(f32)
    return high, mid, rest - mid


def correct_kernel(terms, level_three, restrict, two, basis, first, result, held, sem):
    members, height, lanes = terms.shape
    placed = jnp.concatenate([terms[member] for member in range(members)], axis=0)
    three = dot(level_three[...], placed)
    coarse = two[...] + dot(restrict[...], three)
    c0, c1, c2 = split(coarse)
    right = jnp.concatenate([c0, c1, c2, c0, c1, c0], axis=0).astype(jnp.bfloat16)
    pieces = sem.shape[0]
    cells = held.shape[0] // pieces
    copies = []
    for piece in range(pieces):
        at = pl.ds(piece * cells, cells)
        b0, b1, b2 = split(basis[:, piece * cells : (piece + 1) * cells])
        left = jnp.concatenate([b0, b0, b0, b1, b1, b2], axis=0).T.astype(jnp.bfloat16)
        held[at] = first[at] + jnp.dot(left, right, preferred_element_type=f32)
        copy = pltpu.make_async_copy(held.at[at], result.at[at], sem.at[piece])
        copy.start()
        copies.append(copy)
    for copy in copies:
        copy.wait()


def vmem_call(body, out_shape, inputs, name, scalars=0):
    whole = pl.BlockSpec(memory_space=pltpu.VMEM)
    return pl.pallas_call(
        body,
        out_shape=out_shape,
        in_specs=[pl.BlockSpec(memory_space=pltpu.SMEM)] * scalars + [whole] * (len(inputs) - scalars),
        out_specs=jax.tree.map(lambda _: whole, out_shape),
        compiler_params=pltpu.CompilerParams(vmem_limit_bytes=VMEM_LIMIT),
        name=name,
    )(*inputs)


def shards(
    residual,
    labels,
    region_kappa,
    coarse_basis,
    primal_cells,
    level_two,
    row_restrict,
    level_three,
    row_order,
):
    cells_x, cells_y, rhs_count = residual.shape
    coarse_count = coarse_basis.shape[0]
    cell_count = cells_x * cells_y
    local_two = level_two[0]
    local_restrict = row_restrict[0]
    coarse_third = local_restrict.shape[1]
    members_x, members_y = lax.axis_size("sx"), lax.axis_size("sy")

    first, slack, row_first, row_last, col_first, col_last, root = solve(residual, labels, region_kappa)

    def sent(edge, axis, up):
        count = lax.axis_size(axis)
        pairs = [(i, i + 1) if up else (i + 1, i) for i in range(count - 1)]
        return lax.ppermute(edge, axis, pairs)

    row_low, row_high = sent(row_last, "sx", True), sent(row_first, "sx", False)
    col_low, col_high = sent(col_last, "sy", True), sent(col_first, "sy", False)

    primal = primal_cells.reshape(-1)
    basis_cells = coarse_basis.reshape(coarse_count, cell_count)
    partial = vmem_call(
        inner_kernel,
        jax.ShapeDtypeStruct((coarse_count, rhs_count), f32),
        (primal, basis_cells, slack.reshape(cell_count, rhs_count)),
        "inner",
        scalars=1,
    )
    order_table = (
        row_order[None, :] == jnp.arange(row_order.shape[0], dtype=jnp.int32)[:, None]
    ).astype(f32)
    permuted = jnp.dot(level_three, order_table, precision=highest)

    copies = vmem_call(
        restrict_kernel,
        jax.ShapeDtypeStruct((members_y, coarse_count + coarse_third, rhs_count), f32),
        (
            primal,
            partial,
            basis_cells,
            coarse_basis[:, :, 0],
            coarse_basis[:, :, -1],
            root,
            row_low,
            row_high,
            col_low,
            col_high,
            local_restrict,
            permuted,
        ),
        "restrict",
        scalars=1,
    )
    everyone = lax.all_to_all(copies, "sy", 0, 0, tiled=True)
    two, copies = vmem_call(
        row_kernel,
        (
            jax.ShapeDtypeStruct((coarse_count, rhs_count), f32),
            jax.ShapeDtypeStruct((members_x, coarse_third, rhs_count), f32),
        ),
        (everyone, local_two),
        "row",
    )
    terms = lax.all_to_all(copies, "sx", 0, 0, tiled=True)

    whole = pl.BlockSpec(memory_space=pltpu.VMEM)
    result = pl.pallas_call(
        correct_kernel,
        out_shape=jax.ShapeDtypeStruct((cell_count, rhs_count), f32),
        in_specs=[whole] * 6,
        out_specs=pl.BlockSpec(memory_space=pl.ANY),
        scratch_shapes=[pltpu.VMEM((cell_count, rhs_count), f32), pltpu.SemaphoreType.DMA((6,))],
        compiler_params=pltpu.CompilerParams(vmem_limit_bytes=VMEM_LIMIT),
        name="correct",
    )(terms, permuted, local_restrict, two, basis_cells, first.reshape(cell_count, rhs_count))
    return result.reshape(cells_x, cells_y, rhs_count)


def solution(mesh):
    in_specs = (
        P("sx", "sy", None),
        P("sx", "sy"),
        P(),
        P(None, "sx", "sy"),
        P("sx", "sy", None),
        P("sx", "sy", None),
        P("sx", "sy", None),
        P("sx", None),
        P(),
    )
    out_specs = P("sx", "sy", None)
    return jax.shard_map(shards, mesh=mesh, in_specs=in_specs, out_specs=out_specs, check_vma=False)
```

time: 101 us -> 92.3 us (0.914)
  blocking collectives: 28.5 us -> 55 us
  starting transfers between devices: 37.6 us -> 22.9 us
  waiting for transfers between devices: 15.4 us -> 1.76 us
  other arithmetic: 11.6 us -> 0 us
  Pallas kernels: 0 us -> 8.58 us
  matrix products: 4.13 us -> 0.41 us
    all_to_all x1 -> x2, blocking collectives: 28.5 us -> 55 us  [the longest x1 30.1 us: shards(): terms = lax.all_to_all(copies, 'sx', 0, 0, tiled=True)]
    all_to_all x1 -> x0, waiting for transfers between devices: 14.6 us -> none  [gathered(): return lax.all_to_all(copies, axis, 0, 0, tiled=True)]
    all_to_all x1 -> x0, starting transfers between devices: 14.1 us -> none  [gathered(): return lax.all_to_all(copies, axis, 0, 0, tiled=True)]
    pallas_call x0 -> x5, Pallas kernels: none -> 8.58 us  [the longest x1 4.55 us: solve(): pl.pallas_call(solve_kernel, out_shape=(field, field, edge_x, edge_x, edg...]
    mul x8 -> x0, other arithmetic: 7.97 us -> none  [the longest x7 6.28 us: apply_local(): scaled_in = root_coef * values_in]
    dot_general x7 -> x1, matrix products: 4.13 us -> 0.41 us  [shards(): permuted = jnp.dot(level_three, order_table, precision=highest)]
    unnamed x14 -> x20, local copies, waits for them, and re-layouts: 0.04 us -> 2.91 us
    dot_general x1 -> x0, local copies, waits for them, and re-layouts: 1.63 us -> none  [shards(): lax.dot_general(basis_cells, coarse, (((0,), (0,)), ((), ())), precision=...]
  transfers between devices with their start and end apart: 5 -> 4, of which waited for: 2 -> 1; matrix products, arithmetic and copies ran while one was open for 1% -> 1% of each run, Pallas kernels for 0% -> 1%
where the time goes in v2:
time: 92.3 us; the launch traced here: 92 us
  blocking collectives  55 us (60%)
  starting transfers between devices  22.9 us (25%)
  Pallas kernels  8.58 us (9%)
  local copies, waits for them, and re-layouts  3.15 us (3%)
  waiting for transfers between devices  1.76 us (2%)
    all_to_all x1, blocking collectives, shards(): terms = lax.all_to_all(copies, 'sx', 0, 0, tiled=True)  30.1 us
    all_to_all x1, blocking collectives, shards(): everyone = lax.all_to_all(copies, 'sy', 0, 0, tiled=True)  24.9 us
    ppermute x4, starting transfers between devices, sent(): return lax.ppermute(edge, axis, pairs)  22.9 us
    pallas_call x1, Pallas kernels, solve(): pl.pallas_call(solve_kernel, out_shape=(field, field, edge_x, edge_x, edg...  4.55 us
    unnamed x20, local copies, waits for them, and re-layouts  2.91 us
    pallas_call x3, Pallas kernels, vmem_call(): pl.pallas_call(body, out_shape=out_shape, in_specs=[pl.BlockSpec(memory_s...  2.43 us
  transfers between devices with their start and end apart: 4, of which 1 were waited for; matrix products, arithmetic and copies ran while one was open for 1% of the time, Pallas kernels for 1%

profile of v2, /device:TPU:1, one launch (start us, length us, event | category | flops | bytes accessed | tf_op | source)
XLA Modules:
  0.0 92.0 jit_solution(10423415742497409104)
XLA Ops:
  0.0 0.0 copy-start
  0.0 1.3 %copy-done.1 = f32[48,48,128]{2,1,0:T(8,128)S(1)} copy-done((f32[48,48,128]{2,1,0:T(8,128)S(1)}, f32[48,48,128]{2,1,0:T(8,128)}, u32[]{:S(2)}) %copy-start.1) | copy-done | bytes 1179672
  1.3 0.7 copy-done.2
  2.0 0.7 copy-done.6
  2.7 4.5 %solve.1 = (f32[48,48,128]{2,1,0:T(8,128)S(1)}, f32[48,48,128]{2,1,0:T(8,128)S(1)}, f32[48,128]{1,0:T(8,128)S(1)}, f32[48,128]{1,0:T(8,128)S(1)}, f32[48,128]{1,...) custom-call(f32[8]{0:T(128)S(1)} %copy-done.6, s32[48,48]{1,0:T(8,128)S(1)} %copy-done.2, ...), custom_call_target="tpu_custom_call" | custom-call | flops 23592960 | bytes 3538944 | tf_op jit(solution)/shard_map/solve/pallas_call | solution.py:120
  7.2 15.7 %collective-permute-start = (f32[48,128]{1,0:T(8,128)S(1)}, f32[48,128]{1,0:T(8,128)S(1)}, u32[]{:S(2)}, u32[]{:S(2)}) collective-permute-start(f32[48,128]{1,0:T(8,128)S(1)} %get-tuple-element.16), channel_id=1, source_target_pairs={{0,32},{32,64},{64,96},{96,128},{128,160},{160,192},{192,224},{224... | collective-permute-start | bytes 73736 | tf_op jit(solution)/shard_map/ppermute | solution.py:273
  22.9 1.9 %collective-permute-start.1 = (f32[48,128]{1,0:T(8,128)S(1)}, f32[48,128]{1,0:T(8,128)S(1)}, u32[]{:S(2)}, u32[]{:S(2)}) collective-permute-start(f32[48,128]{1,0:T(8,128)S(1)} %get-tuple-element.17), channel_id=1, source_target_pairs={{32,0},{64,32},{96,64},{128,96},{160,128},{192,160},{224,192},{256... | collective-permute-start | bytes 73736 | tf_op jit(solution)/shard_map/ppermute | solution.py:273
  24.8 4.0 %collective-permute-start.2 = (f32[48,128]{1,0:T(8,128)S(1)}, f32[48,128]{1,0:T(8,128)S(1)}, u32[]{:S(2)}, u32[]{:S(2)}) collective-permute-start(f32[48,128]{1,0:T(8,128)S(1)} %get-tuple-element.18), channel_id=1, source_target_pairs={{0,1},{1,2},{2,3},{3,4},{4,5},{5,6},{6,7},{7,8},{8,9},{9,10},{10,1... | collective-permute-start | bytes 73736 | tf_op jit(solution)/shard_map/ppermute | solution.py:273
  28.8 1.3 %collective-permute-start.3 = (f32[48,128]{1,0:T(8,128)S(1)}, f32[48,128]{1,0:T(8,128)S(1)}, u32[]{:S(2)}, u32[]{:S(2)}) collective-permute-start(f32[48,128]{1,0:T(8,128)S(1)} %get-tuple-element.19), channel_id=1, source_target_pairs={{1,0},{2,1},{3,2},{4,3},{5,4},{6,5},{7,6},{8,7},{9,8},{10,9},{11,1... | collective-permute-start | bytes 73736 | tf_op jit(solution)/shard_map/ppermute | solution.py:273
  30.1 0.0 copy-done.7
  30.1 0.1 fusion.1
  30.3 0.0 copy-done
  30.3 0.0 copy-done.8
  30.3 0.0 copy-start.3
  30.3 0.4 convolution_bitcast_fusion.permuted.level_three
  30.7 0.1 reshape.17.basis
  30.8 0.1 copy.13
  31.0 0.1 copy.12
  31.1 0.0 copy-done.5
  31.1 0.0 copy-start.4
  31.1 1.2 %inner.1.partial = f32[8,128]{1,0:T(8,128)S(1)} custom-call(s32[8]{0:T(128)S(1)} %bitcast.18, f32[8,2304]{1,0:T(8,128)S(1)} %reshape.17.basis, f32[2304,128]{1,0:T(8,128)S(1)} %bitcast.11), custom_call_target="tpu_custom_call" | custom-call | tf_op jit(solution)/shard_map/inner/pallas_call | solution.py:239
  32.3 0.0 collective-permute-done.row_low
  32.3 0.0 collective-permute-done.1.row_high
  32.3 0.0 collective-permute-done.2.col_low
  32.3 1.8 %collective-permute-done.3.col_high = f32[48,128]{1,0:T(8,128)S(1)} collective-permute-done((f32[48,128]{1,0:T(8,128)S(1)}, f32[48,128]{1,0:T(8,128)S(1)}, u32[]{:S(2)}, u32[]{:S(2)}) %collective-permute-start.3) | collective-permute-done | bytes 24608 | tf_op jit(solution)/shard_map/ppermute | solution.py:273
  34.1 0.0 copy-done.3
  34.1 1.1 %restrict.1 = f32[32,24,128]{2,1,0:T(8,128)S(1)} custom-call(s32[8]{0:T(128)S(1)} %bitcast.19, f32[8,128]{1,0:T(8,128)S(1)} %inner.1.partial, f32[8,2304]{1,0:T(8,128)S(1)} %reshape.17.basis, f32[8,48]{1,0:T(8,128)S(1)} %bitcast.16, f32[8,48]{1,0:T(8,128)S(1)} %bitcast.15, f32[48,48]{1,0:T(8,128)S(1)} %get-tuple-element.15.root, ...), custom_call_target="tpu_custom_call" | custom-call | tf_op jit(solution)/shard_map/restrict/pallas_call | solution.py:239
  35.1 24.9 %all_to_all.10.everyone = f32[32,24,128]{2,1,0:T(8,128)S(1)} all-to-all(f32[32,24,128]{2,1,0:T(8,128)S(1)} %restrict.1), channel_id=1, replica_groups=mesh['sx'=32,'sy'=32] {'sy'}, dimensions={0} | all-to-all | bytes 786432 | tf_op jit(solution)/shard_map/all_to_all | solution.py:312
  60.1 0.0 copy-done.4
  60.1 0.2 row.1
  60.2 30.1 %all_to_all.11.terms = f32[32,16,128]{2,1,0:T(8,128)S(1)} all-to-all(f32[32,16,128]{2,1,0:T(8,128)S(1)} %get-tuple-element.20), channel_id=1, replica_groups=mesh['sx'=32,'sy'=32] {'sx'}, dimensions={0} | all-to-all | bytes 524288 | tf_op jit(solution)/shard_map/all_to_all | solution.py:322
  90.3 1.6 %correct.1 = f32[2304,128]{1,0:T(8,128)} custom-call(f32[32,16,128]{2,1,0:T(8,128)S(1)} %all_to_all.11.terms, f32[16,512]{1,0:T(8,128)S(1)} %convolution_bitcast_fusion.permuted.level_three, f32[8,16]{1,0:T(8,128)S(1)} %bitcast.14, f32[8,128]{1,0:T(8,128)S(1)} %get-tuple-element.21.two, f32[8,2304]{1,0:T(8,128)S(1)} %reshape.17.basis, f32[2304,128]{1,0:T(8,128)S(1)} %bitcast.12), custom_call_target="tpu_custom_call" | custom-call | tf_op jit(solution)/shard_map/correct/pallas_call | solution.py:325
  (6 shorter events, 0.0 us)
Async XLA Ops:
  0.0 30.3 %copy-start = (f32[16,512]{1,0:T(8,128)S(1)}, f32[16,512]{1,0:T(8,128)}, u32[]{:S(2)}) copy-start(f32[16,512]{1,0:T(8,128)} %param.16) | copy-start | bytes 98308
  0.0 1.3 %copy-start.1 = (f32[48,48,128]{2,1,0:T(8,128)S(1)}, f32[48,48,128]{2,1,0:T(8,128)}, u32[]{:S(2)}) copy-start(f32[48,48,128]{2,1,0:T(8,128)} %residual.1) | copy-start | bytes 3538948
  1.3 0.7 copy-start.2
  2.0 0.7 copy-start.6
  2.7 27.5 %copy-start.7 = (f32[8,48,48]{2,1,0:T(8,128)S(1)}, f32[8,48,48]{2,1,0:T(8,128)}, u32[]{:S(2)}) copy-start(f32[8,48,48]{2,1,0:T(8,128)} %param.12) | copy-start | bytes 221188
  2.7 27.6 %copy-start.8 = (s32[512]{0:T(512)S(1)}, s32[512]{0:T(512)}, u32[]{:S(2)}) copy-start(s32[512]{0:T(512)} %param.17) | copy-start | bytes 6148
  2.7 28.4 %copy-start.5 = (s32[1,1,8]{2,1,0:T(1,128)S(1)}, s32[1,1,8]{2,1,0:T(1,128)}, u32[]{:S(2)}) copy-start(s32[1,1,8]{2,1,0:T(1,128)} %param.13) | copy-start | bytes 100
  7.2 25.0 %collective-permute-start = (f32[48,128]{1,0:T(8,128)S(1)}, f32[48,128]{1,0:T(8,128)S(1)}, u32[]{:S(2)}, u32[]{:S(2)}) collective-permute-start(f32[48,128]{1,0:T(8,128)S(1)} %get-tuple-element.16), channel_id=1, source_target_pairs={{0,32},{32,64},{64,96},{96,128},{128,160},{160,192},{192,224},{224... | collective-permute-start | bytes 73736 | tf_op jit(solution)/shard_map/ppermute | solution.py:273
  22.9 9.4 %collective-permute-start.1 = (f32[48,128]{1,0:T(8,128)S(1)}, f32[48,128]{1,0:T(8,128)S(1)}, u32[]{:S(2)}, u32[]{:S(2)}) collective-permute-start(f32[48,128]{1,0:T(8,128)S(1)} %get-tuple-element.17), channel_id=1, source_target_pairs={{32,0},{64,32},{96,64},{128,96},{160,128},{192,160},{224,192},{256... | collective-permute-start | bytes 73736 | tf_op jit(solution)/shard_map/ppermute | solution.py:273
  24.8 7.5 %collective-permute-start.2 = (f32[48,128]{1,0:T(8,128)S(1)}, f32[48,128]{1,0:T(8,128)S(1)}, u32[]{:S(2)}, u32[]{:S(2)}) collective-permute-start(f32[48,128]{1,0:T(8,128)S(1)} %get-tuple-element.18), channel_id=1, source_target_pairs={{0,1},{1,2},{2,3},{3,4},{4,5},{5,6},{6,7},{7,8},{8,9},{9,10},{10,1... | collective-permute-start | bytes 73736 | tf_op jit(solution)/shard_map/ppermute | solution.py:273
  28.8 5.2 %collective-permute-start.3 = (f32[48,128]{1,0:T(8,128)S(1)}, f32[48,128]{1,0:T(8,128)S(1)}, u32[]{:S(2)}, u32[]{:S(2)}) collective-permute-start(f32[48,128]{1,0:T(8,128)S(1)} %get-tuple-element.19), channel_id=1, source_target_pairs={{1,0},{2,1},{3,2},{4,3},{5,4},{6,5},{7,6},{8,7},{9,8},{10,9},{11,1... | collective-permute-start | bytes 73736 | tf_op jit(solution)/shard_map/ppermute | solution.py:273
  30.3 3.8 %copy-start.3 = (f32[1,8,16]{2,1,0:T(8,128)S(1)}, f32[1,8,16]{2,1,0:T(8,128)}, u32[]{:S(2)}) copy-start(f32[1,8,16]{2,1,0:T(8,128)} %param.15) | copy-start | bytes 1540
  31.1 29.0 %copy-start.4 = (f32[1,8,256]{2,1,0:T(8,128)S(1)}, f32[1,8,256]{2,1,0:T(8,128)}, u32[]{:S(2)}) copy-start(f32[1,8,256]{2,1,0:T(8,128)} %param.14) | copy-start | bytes 24580

commit v3 on v2

--- a/solution.py
+++ b/solution.py
@@ -34,28 +34,40 @@
 
 
 def solve_kernel(
-    kappa,
+    kappa_hbm,
     labels,
     residual,
     first,
     slack,
-    row_first,
-    row_last,
-    col_first,
-    col_last,
+    row_far,
+    row_near,
+    col_far,
+    col_near,
     root_out,
     zs,
     wide,
     rhs,
     coef,
+    loaded,
+    kinds,
+    kappa,
+    load_sem,
 ):
     n, m = labels.shape
-    here = labels[...]
-    kap = jnp.full(here.shape, kappa[0], f32)
-    for region in range(1, kappa.shape[0]):
-        kap = jnp.where(here == region, kappa[region], kap)
-    root_out[...] = jnp.sqrt(kap)
-    kap_t = kap.T
+    parts = load_sem.shape[0] - 2
+    rows = n // parts
+    kinds_copy = pltpu.make_async_copy(labels, kinds, load_sem.at[parts])
+    kinds_copy.start()
+    kappa_copy = pltpu.make_async_copy(kappa_hbm, kappa, load_sem.at[parts + 1])
+    kappa_copy.start()
+    loads = [
+        pltpu.make_async_copy(
+            residual.at[pl.ds(p * rows, rows)], loaded.at[pl.ds(p * rows, rows)], load_sem.at[p]
+        )
+        for p in range(parts)
+    ]
+    for copy in loads:
+        copy.start()
     scale, factors = sweep_factors()
     lanes = residual.shape[2]
     zero_row = jnp.zeros((8, lanes), f32)
@@ -66,10 +78,20 @@
             buffer[i, 0:8] = zero_row
             buffer[i, 8 + m :] = zero_row
 
+    kinds_copy.wait()
+    kappa_copy.wait()
+    here = kinds[...]
+    kap = jnp.full(here.shape, kappa[0], f32)
+    for region in range(1, kappa.shape[0]):
+        kap = jnp.where(here == region, kappa[region], kap)
+    root_out[...] = jnp.sqrt(kap)
+    kap_t = kap.T
     for i in range(n):
+        if i % rows == 0:
+            loads[i // rows].wait()
         spread = jnp.broadcast_to(kap_t[:, i : i + 1], (m, lanes))
         coef[i] = spread
-        rhs[i + 1, 8 : 8 + m] = (spread * lax.rsqrt(spread)) * residual[i]
+        rhs[i + 1, 8 : 8 + m] = (spread * lax.rsqrt(spread)) * loaded[i]
 
     def neighbours(source, i, before, here_row):
         after = source[i + 2, 8 : 8 + m]
@@ -99,16 +121,22 @@
         lax.fori_loop(0, n // unroll, some_rows, (jnp.zeros((m, lanes), f32), source[1, 8 : 8 + m]))
 
     before, here_row = jnp.zeros((m, lanes), f32), zs[1, 8 : 8 + m]
-    row_first[...] = here_row
-    row_last[...] = zs[n, 8 : 8 + m]
+    even_x = lax.rem(lax.axis_index("sx"), 2) == 0
+    even_y = lax.rem(lax.axis_index("sy"), 2) == 0
+    row_last = zs[n, 8 : 8 + m]
+    row_far[...] = jnp.where(even_x, here_row, row_last)
+    row_near[...] = jnp.where(even_x, row_last, here_row)
     for i in range(n):
         after, product = neighbours(zs, i, before, here_row)
         inv = lax.rsqrt(coef[i])
         slack[i] = (rhs[i + 1, 8 : 8 + m] + product) * inv
         first[i] = here_row * inv
-        col_first[i : i + 1] = here_row[0:1]
-        col_last[i : i + 1] = here_row[m - 1 : m]
+        col_far[i : i + 1] = here_row[0:1]
+        col_near[i : i + 1] = here_row[m - 1 : m]
         before, here_row = here_row, after
+    col_first, col_last = col_far[...], col_near[...]
+    col_far[...] = jnp.where(even_y, col_first, col_last)
+    col_near[...] = jnp.where(even_y, col_last, col_first)
 
 
 def solve(residual, labels, region_kappa):
@@ -121,9 +149,9 @@
         solve_kernel,
         out_shape=(field, field, edge_x, edge_x, edge_y, edge_y, jax.ShapeDtypeStruct((n, m), f32)),
         in_specs=[
-            pl.BlockSpec(memory_space=pltpu.SMEM),
-            whole,
-            whole,
+            pl.BlockSpec(memory_space=pltpu.HBM),
+            pl.BlockSpec(memory_space=pltpu.HBM),
+            pl.BlockSpec(memory_space=pltpu.HBM),
         ],
         out_specs=[whole] * 7,
         scratch_shapes=[
@@ -131,13 +159,21 @@
             pltpu.VMEM((n, m, lanes), f32),
             pltpu.VMEM((n + 2, m + 16, lanes), f32),
             pltpu.VMEM((n, m, lanes), f32),
+            pltpu.VMEM((n, m, lanes), f32),
+            pltpu.VMEM((n, m), jnp.int32),
+            pltpu.SMEM(region_kappa.shape, f32),
+            pltpu.SemaphoreType.DMA((6,)),
         ],
         compiler_params=pltpu.CompilerParams(vmem_limit_bytes=VMEM_LIMIT),
         cost_estimate=pl.CostEstimate(
             flops=80 * n * m * lanes, bytes_accessed=12 * n * m * lanes, transcendentals=0
         ),
         name="solve",
-    )(region_kappa, labels, residual)
+    )(
+        pltpu.with_memory_space_constraint(region_kappa, pltpu.HBM),
+        pltpu.with_memory_space_constraint(labels, pltpu.HBM),
+        pltpu.with_memory_space_constraint(residual, pltpu.HBM),
+    )
 
 
 def chosen_cells(primal, width):
@@ -161,15 +197,21 @@
     basis_first,
     basis_last,
     root,
-    row_low,
-    row_high,
-    col_low,
-    col_high,
+    row_far,
+    row_near,
+    col_far,
+    col_near,
     restrict,
     permuted,
     out,
 ):
     n, m = root.shape
+    even_x = lax.rem(lax.axis_index("sx"), 2) == 0
+    even_y = lax.rem(lax.axis_index("sy"), 2) == 0
+    row_low = jnp.where(even_x, row_far[...], row_near[...])
+    row_high = jnp.where(even_x, row_near[...], row_far[...])
+    col_low = jnp.where(even_y, col_far[...], col_near[...])
+    col_high = jnp.where(even_y, col_near[...], col_far[...])
     here = root[...]
     turned = here.T
     last = (n - 1) * m
@@ -177,7 +219,7 @@
     def share(weights, begin, stride, scale, halo):
         cell = begin + stride * lax.broadcasted_iota(jnp.int32, weights.shape, 1)
         weights = weights + jnp.where(cell == chosen_cells(primal, weights.shape[1]), 1.0, 0.0)
-        return dot(weights * scale, halo[...])
+        return dot(weights * scale, halo)
 
     coarse_res = (
         partial[...]
@@ -265,15 +307,17 @@
     coarse_third = local_restrict.shape[1]
     members_x, members_y = lax.axis_size("sx"), lax.axis_size("sy")
 
-    first, slack, row_first, row_last, col_first, col_last, root = solve(residual, labels, region_kappa)
-
-    def sent(edge, axis, up):
+    first, slack, row_far, row_near, col_far, col_near, root = solve(residual, labels, region_kappa)
+
+    def swapped(edge, axis, begin):
         count = lax.axis_size(axis)
-        pairs = [(i, i + 1) if up else (i + 1, i) for i in range(count - 1)]
-        return lax.ppermute(edge, axis, pairs)
-
-    row_low, row_high = sent(row_last, "sx", True), sent(row_first, "sx", False)
-    col_low, col_high = sent(col_last, "sy", True), sent(col_first, "sy", False)
+        pairs = [(i, i + 1) for i in range(begin, count - 1, 2)]
+        return lax.ppermute(edge, axis, pairs + [(target, source) for source, target in pairs])
+
+    row_far = swapped(row_far, "sx", 1)
+    col_far = swapped(col_far, "sy", 1)
+    row_near = swapped(row_near, "sx", 0)
+    col_near = swapped(col_near, "sy", 0)
 
     primal = primal_cells.reshape(-1)
     basis_cells = coarse_basis.reshape(coarse_count, cell_count)
@@ -299,10 +343,10 @@
             coarse_basis[:, :, 0],
             coarse_basis[:, :, -1],
             root,
-            row_low,
-            row_high,
-            col_low,
-            col_high,
+            row_far,
+            row_near,
+            col_far,
+            col_near,
             local_restrict,
             permuted,
         ),

time: 92.3 us -> 85.2 us (0.923)
  blocking collectives: 55 us -> 49 us
  starting transfers between devices: 22.9 us -> 25.6 us
  local copies, waits for them, and re-layouts: 3.15 us -> 0.48 us
  waiting for transfers between devices: 1.76 us -> 0.02 us
    all_to_all x1, blocking collectives: 30.1 us -> 25.4 us  [shards(): terms = lax.all_to_all(copies, 'sx', 0, 0, tiled=True)]
    ppermute x4, starting transfers between devices: 22.9 us -> 25.6 us  [swapped(): lax.ppermute(edge, axis, pairs + [(target, source) for source, target in...]
    unnamed x20 -> x14, local copies, waits for them, and re-layouts: 2.91 us -> 0.24 us
    ppermute x4, waiting for transfers between devices: 1.76 us -> 0.02 us  [swapped(): lax.ppermute(edge, axis, pairs + [(target, source) for source, target in...]
    all_to_all x1, blocking collectives: 24.9 us -> 23.6 us  [shards(): everyone = lax.all_to_all(copies, 'sy', 0, 0, tiled=True)]
  transfers between devices with their start and end apart: 4 -> 4, of which waited for: 1 -> 0; matrix products, arithmetic and copies ran while one was open for 1% -> 1% of each run, Pallas kernels for 1% -> 1%
where the time goes in v3:
time: 85.2 us; the launch traced here: 85 us
  blocking collectives  49 us (58%)
  starting transfers between devices  25.6 us (30%)
  Pallas kernels  9.25 us (11%)
    ppermute x4, starting transfers between devices, swapped(): lax.ppermute(edge, axis, pairs + [(target, source) for source, target in...  25.6 us
    all_to_all x1, blocking collectives, shards(): terms = lax.all_to_all(copies, 'sx', 0, 0, tiled=True)  25.4 us
    all_to_all x1, blocking collectives, shards(): everyone = lax.all_to_all(copies, 'sy', 0, 0, tiled=True)  23.6 us
    pallas_call x1, Pallas kernels, solve(): pl.pallas_call(solve_kernel, out_shape=(field, field, edge_x, edge_x, edg...  5.21 us
    pallas_call x3, Pallas kernels, vmem_call(): pl.pallas_call(body, out_shape=out_shape, in_specs=[pl.BlockSpec(memory_s...  2.43 us
  transfers between devices with their start and end apart: 4, of which 0 were waited for; matrix products, arithmetic and copies ran while one was open for 1% of the time, Pallas kernels for 1%

profile of v3, /device:TPU:1, one launch (start us, length us, event | category | flops | bytes accessed | tf_op | source)
XLA Modules:
  0.0 85.0 jit_solution(10622048546283833092)
XLA Ops:
  0.0 0.0 copy-start
  0.0 0.0 copy-start.4
  0.0 0.0 copy-start.5
  0.0 0.0 copy-start.3
  0.0 5.2 %solve.1 = (f32[48,48,128]{2,1,0:T(8,128)S(1)}, f32[48,48,128]{2,1,0:T(8,128)S(1)}, f32[48,128]{1,0:T(8,128)S(1)}, f32[48,128]{1,0:T(8,128)S(1)}, f32[48,128]{1,...) custom-call(f32[8]{0:T(128)} %kappa_hbm.1, s32[48,48]{1,0:T(8,128)} %labels.1, f32[48,48,128]{2,1,0:T(8,128)} %residual.1), custom_call_target="tpu_custom_call" | custom-call | flops 23592960 | bytes 3538944 | tf_op jit(solution)/shard_map/solve/pallas_call | solution.py:148
  5.2 15.7 %collective-permute-start = (f32[48,128]{1,0:T(8,128)S(1)}, f32[48,128]{1,0:T(8,128)S(1)}, u32[]{:S(2)}, u32[]{:S(2)}) collective-permute-start(f32[48,128]{1,0:T(8,128)S(1)} %get-tuple-element.16), channel_id=1, source_target_pairs={{32,64},{96,128},{160,192},{224,256},{288,320},{352,384},{416,448}... | collective-permute-start | bytes 73736 | tf_op jit(solution)/shard_map/ppermute | solution.py:315
  20.9 1.9 %collective-permute-start.1 = (f32[48,128]{1,0:T(8,128)S(1)}, f32[48,128]{1,0:T(8,128)S(1)}, u32[]{:S(2)}, u32[]{:S(2)}) collective-permute-start(f32[48,128]{1,0:T(8,128)S(1)} %get-tuple-element.17), channel_id=1, source_target_pairs={{0,32},{64,96},{128,160},{192,224},{256,288},{320,352},{384,416},{... | collective-permute-start | bytes 73736 | tf_op jit(solution)/shard_map/ppermute | solution.py:315
  22.8 0.7 collective-permute-start.2
  23.5 7.4 %collective-permute-start.3 = (f32[48,128]{1,0:T(8,128)S(1)}, f32[48,128]{1,0:T(8,128)S(1)}, u32[]{:S(2)}, u32[]{:S(2)}) collective-permute-start(f32[48,128]{1,0:T(8,128)S(1)} %get-tuple-element.19), channel_id=1, source_target_pairs={{0,1},{2,3},{4,5},{6,7},{8,9},{10,11},{12,13},{14,15},{16,17},{18,... | collective-permute-start | bytes 73736 | tf_op jit(solution)/shard_map/ppermute | solution.py:315
  30.9 0.0 copy-done.4
  30.9 0.1 fusion.1
  31.0 0.0 copy-done
  31.0 0.0 copy-done.5
  31.0 0.0 copy-start.1
  31.0 0.4 convolution_bitcast_fusion.permuted.level_three
  31.4 0.1 reshape.17.basis
  31.6 0.1 copy.13
  31.7 0.1 copy.12
  31.8 0.0 copy-done.3
  31.8 0.0 copy-start.2
  31.8 1.2 %inner.1.partial = f32[8,128]{1,0:T(8,128)S(1)} custom-call(s32[8]{0:T(128)S(1)} %bitcast.18, f32[8,2304]{1,0:T(8,128)S(1)} %reshape.17.basis, f32[2304,128]{1,0:T(8,128)S(1)} %bitcast.11), custom_call_target="tpu_custom_call" | custom-call | tf_op jit(solution)/shard_map/inner/pallas_call | solution.py:281
  33.0 0.0 collective-permute-done.row_far
  33.0 0.0 collective-permute-done.1.row_near
  33.0 0.0 collective-permute-done.2.col_far
  33.0 0.0 collective-permute-done.3.col_near
  33.0 0.0 copy-done.1
  33.1 1.1 %restrict.1 = f32[32,24,128]{2,1,0:T(8,128)S(1)} custom-call(s32[8]{0:T(128)S(1)} %bitcast.19, f32[8,128]{1,0:T(8,128)S(1)} %inner.1.partial, f32[8,2304]{1,0:T(8,128)S(1)} %reshape.17.basis, f32[8,48]{1,0:T(8,128)S(1)} %bitcast.16, f32[8,48]{1,0:T(8,128)S(1)} %bitcast.15, f32[48,48]{1,0:T(8,128)S(1)} %get-tuple-element.15.root, ...), custom_call_target="tpu_custom_call" | custom-call | tf_op jit(solution)/shard_map/restrict/pallas_call | solution.py:281
  34.1 23.6 %all_to_all.10.everyone = f32[32,24,128]{2,1,0:T(8,128)S(1)} all-to-all(f32[32,24,128]{2,1,0:T(8,128)S(1)} %restrict.1), channel_id=1, replica_groups=mesh['sx'=32,'sy'=32] {'sy'}, dimensions={0} | all-to-all | bytes 786432 | tf_op jit(solution)/shard_map/all_to_all | solution.py:356
  57.7 0.0 copy-done.2
  57.7 0.2 row.1
  57.9 25.4 %all_to_all.11.terms = f32[32,16,128]{2,1,0:T(8,128)S(1)} all-to-all(f32[32,16,128]{2,1,0:T(8,128)S(1)} %get-tuple-element.20), channel_id=1, replica_groups=mesh['sx'=32,'sy'=32] {'sx'}, dimensions={0} | all-to-all | bytes 524288 | tf_op jit(solution)/shard_map/all_to_all | solution.py:366
  83.4 1.6 %correct.1 = f32[2304,128]{1,0:T(8,128)} custom-call(f32[32,16,128]{2,1,0:T(8,128)S(1)} %all_to_all.11.terms, f32[16,512]{1,0:T(8,128)S(1)} %convolution_bitcast_fusion.permuted.level_three, f32[8,16]{1,0:T(8,128)S(1)} %bitcast.14, f32[8,128]{1,0:T(8,128)S(1)} %get-tuple-element.21.two, f32[8,2304]{1,0:T(8,128)S(1)} %reshape.17.basis, f32[2304,128]{1,0:T(8,128)S(1)} %bitcast.12), custom_call_target="tpu_custom_call" | custom-call | tf_op jit(solution)/shard_map/correct/pallas_call | solution.py:369
Async XLA Ops:
  0.0 31.0 %copy-start = (f32[16,512]{1,0:T(8,128)S(1)}, f32[16,512]{1,0:T(8,128)}, u32[]{:S(2)}) copy-start(f32[16,512]{1,0:T(8,128)} %param.16) | copy-start | bytes 98308
  0.0 30.9 %copy-start.4 = (f32[8,48,48]{2,1,0:T(8,128)S(1)}, f32[8,48,48]{2,1,0:T(8,128)}, u32[]{:S(2)}) copy-start(f32[8,48,48]{2,1,0:T(8,128)} %param.12) | copy-start | bytes 221188
  0.0 31.0 %copy-start.5 = (s32[512]{0:T(512)S(1)}, s32[512]{0:T(512)}, u32[]{:S(2)}) copy-start(s32[512]{0:T(512)} %param.17) | copy-start | bytes 6148
  0.0 31.8 %copy-start.3 = (s32[1,1,8]{2,1,0:T(1,128)S(1)}, s32[1,1,8]{2,1,0:T(1,128)}, u32[]{:S(2)}) copy-start(s32[1,1,8]{2,1,0:T(1,128)} %param.13) | copy-start | bytes 100
  5.2 27.8 %collective-permute-start = (f32[48,128]{1,0:T(8,128)S(1)}, f32[48,128]{1,0:T(8,128)S(1)}, u32[]{:S(2)}, u32[]{:S(2)}) collective-permute-start(f32[48,128]{1,0:T(8,128)S(1)} %get-tuple-element.16), channel_id=1, source_target_pairs={{32,64},{96,128},{160,192},{224,256},{288,320},{352,384},{416,448}... | collective-permute-start | bytes 73736 | tf_op jit(solution)/shard_map/ppermute | solution.py:315
  20.9 12.1 %collective-permute-start.1 = (f32[48,128]{1,0:T(8,128)S(1)}, f32[48,128]{1,0:T(8,128)S(1)}, u32[]{:S(2)}, u32[]{:S(2)}) collective-permute-start(f32[48,128]{1,0:T(8,128)S(1)} %get-tuple-element.17), channel_id=1, source_target_pairs={{0,32},{64,96},{128,160},{192,224},{256,288},{320,352},{384,416},{... | collective-permute-start | bytes 73736 | tf_op jit(solution)/shard_map/ppermute | solution.py:315
  22.8 10.2 %collective-permute-start.2 = (f32[48,128]{1,0:T(8,128)S(1)}, f32[48,128]{1,0:T(8,128)S(1)}, u32[]{:S(2)}, u32[]{:S(2)}) collective-permute-start(f32[48,128]{1,0:T(8,128)S(1)} %get-tuple-element.18), channel_id=1, source_target_pairs={{1,2},{3,4},{5,6},{7,8},{9,10},{11,12},{13,14},{15,16},{17,18},{19... | collective-permute-start | bytes 73736 | tf_op jit(solution)/shard_map/ppermute | solution.py:315
  23.5 9.5 %collective-permute-start.3 = (f32[48,128]{1,0:T(8,128)S(1)}, f32[48,128]{1,0:T(8,128)S(1)}, u32[]{:S(2)}, u32[]{:S(2)}) collective-permute-start(f32[48,128]{1,0:T(8,128)S(1)} %get-tuple-element.19), channel_id=1, source_target_pairs={{0,1},{2,3},{4,5},{6,7},{8,9},{10,11},{12,13},{14,15},{16,17},{18,... | collective-permute-start | bytes 73736 | tf_op jit(solution)/shard_map/ppermute | solution.py:315
  31.0 2.0 %copy-start.1 = (f32[1,8,16]{2,1,0:T(8,128)S(1)}, f32[1,8,16]{2,1,0:T(8,128)}, u32[]{:S(2)}) copy-start(f32[1,8,16]{2,1,0:T(8,128)} %param.15) | copy-start | bytes 1540
  31.8 25.9 %copy-start.2 = (f32[1,8,256]{2,1,0:T(8,128)S(1)}, f32[1,8,256]{2,1,0:T(8,128)}, u32[]{:S(2)}) copy-start(f32[1,8,256]{2,1,0:T(8,128)} %param.14) | copy-start | bytes 24580

commit v4 on v3

--- a/solution.py
+++ b/solution.py
@@ -40,8 +40,8 @@
     first,
     slack,
     row_far,
+    col_far,
     row_near,
-    col_far,
     col_near,
     root_out,
     zs,
@@ -147,7 +147,7 @@
     whole = pl.BlockSpec(memory_space=pltpu.VMEM)
     return pl.pallas_call(
         solve_kernel,
-        out_shape=(field, field, edge_x, edge_x, edge_y, edge_y, jax.ShapeDtypeStruct((n, m), f32)),
+        out_shape=(field, field, edge_x, edge_y, edge_x, edge_y, jax.ShapeDtypeStruct((n, m), f32)),
         in_specs=[
             pl.BlockSpec(memory_space=pltpu.HBM),
             pl.BlockSpec(memory_space=pltpu.HBM),
@@ -198,8 +198,8 @@
     basis_last,
     root,
     row_far,
+    col_far,
     row_near,
-    col_far,
     col_near,
     restrict,
     permuted,
@@ -216,33 +216,47 @@
     turned = here.T
     last = (n - 1) * m
 
-    def share(weights, begin, stride, scale, halo):
+    def share(weights, begin, stride, scale):
         cell = begin + stride * lax.broadcasted_iota(jnp.int32, weights.shape, 1)
-        weights = weights + jnp.where(cell == chosen_cells(primal, weights.shape[1]), 1.0, 0.0)
-        return dot(weights * scale, halo)
-
-    coarse_res = (
-        partial[...]
-        + (share(basis[:, 0:m], 0, 1, here[0:1], row_low) + share(basis[:, last:], last, 1, here[n - 1 :], row_high))
-        + (
-            share(basis_first[...], 0, m, turned[0:1], col_low)
-            + share(basis_last[...], m - 1, m, turned[m - 1 :], col_high)
-        )
-    )
-    terms = dot(restrict[...], coarse_res, ((0,), (0,)))
-    both = jnp.concatenate([coarse_res, terms], axis=0)
-    for member in range(out.shape[0]):
-        out[member] = both
+        chosen = jnp.where(cell == chosen_cells(primal, weights.shape[1]), 1.0, 0.0)
+        return (weights + chosen) * scale
+
+    weights = jnp.concatenate(
+        [
+            share(basis[:, 0:m], 0, 1, here[0:1]),
+            share(basis[:, last:], last, 1, here[n - 1 :]),
+            share(basis_first[...], 0, m, turned[0:1]),
+            share(basis_last[...], m - 1, m, turned[m - 1 :]),
+        ],
+        axis=1,
+    )
+    halo = jnp.concatenate([row_low, row_high, col_low, col_high], axis=0)
+    both = jnp.concatenate([partial[...] + dot(weights, halo), restrict[...]], axis=0)
+    height = both.shape[0]
+    for member in range(out.shape[0] // height):
+        out[member * height : (member + 1) * height] = both
 
 
 def row_kernel(everyone, local_two, two, out):
-    members, height, lanes = everyone.shape
     count = two.shape[0]
-    values = jnp.concatenate([everyone[member, 0:count] for member in range(members)], axis=0)
+    height = count + 1
+    third = out.shape[1]
+    members = everyone.shape[0] // height
+    values = jnp.concatenate([everyone[m * height : m * height + count] for m in range(members)], axis=0)
     two[...] = dot(local_two[...], values)
-    terms = everyone[0, count:]
-    for member in range(1, members):
-        terms = terms + everyone[member, count:]
+    shape = (count, everyone.shape[1])
+    own = lax.broadcasted_iota(jnp.int32, shape, 1) // third == lax.broadcasted_iota(jnp.int32, shape, 0)
+    spread = jnp.concatenate(
+        [
+            jnp.where(own, jnp.broadcast_to(everyone[m * height + count : (m + 1) * height], shape), 0.0)
+            for m in range(members)
+        ],
+        axis=0,
+    )
+    products = dot(spread, values, ((0,), (0,)))
+    terms = products[0:third]
+    for k in range(1, count):
+        terms = terms + products[k * third : (k + 1) * third]
     for member in range(out.shape[0]):
         out[member] = terms
 
@@ -307,7 +321,7 @@
     coarse_third = local_restrict.shape[1]
     members_x, members_y = lax.axis_size("sx"), lax.axis_size("sy")
 
-    first, slack, row_far, row_near, col_far, col_near, root = solve(residual, labels, region_kappa)
+    first, slack, row_far, col_far, row_near, col_near, root = solve(residual, labels, region_kappa)
 
     def swapped(edge, axis, begin):
         count = lax.axis_size(axis)
@@ -335,7 +349,7 @@
 
     copies = vmem_call(
         restrict_kernel,
-        jax.ShapeDtypeStruct((members_y, coarse_count + coarse_third, rhs_count), f32),
+        jax.ShapeDtypeStruct((members_y * (coarse_count + 1), rhs_count), f32),
         (
             primal,
             partial,
@@ -344,16 +358,16 @@
             coarse_basis[:, :, -1],
             root,
             row_far,
+            col_far,
             row_near,
-            col_far,
             col_near,
-            local_restrict,
+            local_restrict.reshape(1, coarse_count * coarse_third),
             permuted,
         ),
         "restrict",
         scalars=1,
     )
-    everyone = lax.all_to_all(copies, "sy", 0, 0, tiled=True)
+    everyone = lax.all_to_all(copies[:, None], "sy", 0, 0, tiled=True)[:, 0]
     two, copies = vmem_call(
         row_kernel,
         (

time: 85.2 us -> 80.9 us (0.950)
  blocking collectives: 49 us -> 44.6 us
    all_to_all x1, blocking collectives: 23.6 us -> 20.2 us  [shards(): everyone = lax.all_to_all(copies[:, None], 'sy', 0, 0, tiled=True)[:, 0]]
    all_to_all x1, blocking collectives: 25.4 us -> 24.4 us  [shards(): terms = lax.all_to_all(copies, 'sx', 0, 0, tiled=True)]
where the time goes in v4:
time: 80.9 us; the launch traced here: 80.6 us
  blocking collectives  44.6 us (55%)
  starting transfers between devices  25.6 us (32%)
  Pallas kernels  9.23 us (11%)
    ppermute x4, starting transfers between devices, swapped(): lax.ppermute(edge, axis, pairs + [(target, source) for source, target in...  25.6 us
    all_to_all x1, blocking collectives, shards(): terms = lax.all_to_all(copies, 'sx', 0, 0, tiled=True)  24.4 us
    all_to_all x1, blocking collectives, shards(): everyone = lax.all_to_all(copies[:, None], 'sy', 0, 0, tiled=True)[:, 0]  20.2 us
    pallas_call x1, Pallas kernels, solve(): pl.pallas_call(solve_kernel, out_shape=(field, field, edge_x, edge_y, edg...  5.22 us
    pallas_call x3, Pallas kernels, vmem_call(): pl.pallas_call(body, out_shape=out_shape, in_specs=[pl.BlockSpec(memory_s...  2.4 us
  transfers between devices with their start and end apart: 4, of which 0 were waited for; matrix products, arithmetic and copies ran while one was open for 1% of the time, Pallas kernels for 1%

profile of v4, /device:TPU:1, one launch (start us, length us, event | category | flops | bytes accessed | tf_op | source)
XLA Modules:
  0.0 80.6 jit_solution(2533327427067349535)
XLA Ops:
  0.0 0.0 copy-start
  0.0 0.0 copy-start.4
  0.0 0.0 copy-start.5
  0.0 0.0 copy-start.1
  0.0 0.0 copy-start.3
  0.0 5.2 %solve.1 = (f32[48,48,128]{2,1,0:T(8,128)S(1)}, f32[48,48,128]{2,1,0:T(8,128)S(1)}, f32[48,128]{1,0:T(8,128)S(1)}, f32[48,128]{1,0:T(8,128)S(1)}, f32[48,128]{1,...) custom-call(f32[8]{0:T(128)} %kappa_hbm.1, s32[48,48]{1,0:T(8,128)} %labels.1, f32[48,48,128]{2,1,0:T(8,128)} %residual.1), custom_call_target="tpu_custom_call" | custom-call | flops 23592960 | bytes 3538944 | tf_op jit(solution)/shard_map/solve/pallas_call | solution.py:148
  5.3 15.7 %collective-permute-start = (f32[48,128]{1,0:T(8,128)S(1)}, f32[48,128]{1,0:T(8,128)S(1)}, u32[]{:S(2)}, u32[]{:S(2)}) collective-permute-start(f32[48,128]{1,0:T(8,128)S(1)} %get-tuple-element.16), channel_id=1, source_target_pairs={{32,64},{96,128},{160,192},{224,256},{288,320},{352,384},{416,448}... | collective-permute-start | bytes 73736 | tf_op jit(solution)/shard_map/ppermute | solution.py:329
  20.9 0.7 collective-permute-start.1
  21.6 1.9 %collective-permute-start.2 = (f32[48,128]{1,0:T(8,128)S(1)}, f32[48,128]{1,0:T(8,128)S(1)}, u32[]{:S(2)}, u32[]{:S(2)}) collective-permute-start(f32[48,128]{1,0:T(8,128)S(1)} %get-tuple-element.18), channel_id=1, source_target_pairs={{0,32},{64,96},{128,160},{192,224},{256,288},{320,352},{384,416},{... | collective-permute-start | bytes 73736 | tf_op jit(solution)/shard_map/ppermute | solution.py:329
  23.5 7.4 %collective-permute-start.3 = (f32[48,128]{1,0:T(8,128)S(1)}, f32[48,128]{1,0:T(8,128)S(1)}, u32[]{:S(2)}, u32[]{:S(2)}) collective-permute-start(f32[48,128]{1,0:T(8,128)S(1)} %get-tuple-element.19), channel_id=1, source_target_pairs={{0,1},{2,3},{4,5},{6,7},{8,9},{10,11},{12,13},{14,15},{16,17},{18,... | collective-permute-start | bytes 73736 | tf_op jit(solution)/shard_map/ppermute | solution.py:329
  30.9 0.0 copy-done.4
  30.9 0.1 fusion.1
  31.0 0.0 copy-done
  31.0 0.0 copy-done.5
  31.0 0.4 convolution_bitcast_fusion.permuted.level_three
  31.4 0.1 reshape.17.basis
  31.6 0.0 copy-done.1
  31.6 0.1 reshape_squeeze.3.restrict
  31.7 0.1 copy.16
  31.8 0.1 copy.15
  31.9 0.0 copy-done.3
  31.9 1.2 %inner.1.partial = f32[8,128]{1,0:T(8,128)S(1)} custom-call(s32[8]{0:T(128)S(1)} %bitcast.23, f32[8,2304]{1,0:T(8,128)S(1)} %reshape.17.basis, f32[2304,128]{1,0:T(8,128)S(1)} %bitcast.15), custom_call_target="tpu_custom_call" | custom-call | tf_op jit(solution)/shard_map/inner/pallas_call | solution.py:295
  33.1 0.0 collective-permute-done.row_far
  33.1 0.0 collective-permute-done.1.col_far
  33.1 0.0 collective-permute-done.2.row_near
  33.1 0.0 collective-permute-done.3.col_near
  33.1 0.9 %restrict.1 = f32[288,128]{1,0:T(8,128)S(1)} custom-call(s32[8]{0:T(128)S(1)} %bitcast.24, f32[8,128]{1,0:T(8,128)S(1)} %inner.1.partial, f32[8,2304]{1,0:T(8,128)S(1)} %reshape.17.basis, f32[8,48]{1,0:T(8,128)S(1)} %bitcast.20, f32[8,48]{1,0:T(8,128)S(1)} %bitcast.19, f32[48,48]{1,0:T(8,128)S(1)} %get-tuple-element.15.root, ...), custom_call_target="tpu_custom_call" | custom-call | tf_op jit(solution)/shard_map/restrict/pallas_call | solution.py:295
  34.0 20.2 %all_to_all.10 = f32[288,1,128]{2,1,0:T(1,128)S(1)} all-to-all(f32[288,1,128]{2,1,0:T(1,128)S(1)} %bitcast.17), channel_id=1, replica_groups=mesh['sx'=32,'sy'=32] {'sy'}, dimensions={0} | all-to-all | bytes 294912 | tf_op jit(solution)/shard_map/all_to_all | solution.py:370
  54.3 0.0 copy-done.2
  54.3 0.3 row.1
  54.6 24.4 %all_to_all.11.terms = f32[32,16,128]{2,1,0:T(8,128)S(1)} all-to-all(f32[32,16,128]{2,1,0:T(8,128)S(1)} %get-tuple-element.20), channel_id=1, replica_groups=mesh['sx'=32,'sy'=32] {'sx'}, dimensions={0} | all-to-all | bytes 524288 | tf_op jit(solution)/shard_map/all_to_all | solution.py:380
  79.0 1.6 %correct.1 = f32[2304,128]{1,0:T(8,128)} custom-call(f32[32,16,128]{2,1,0:T(8,128)S(1)} %all_to_all.11.terms, f32[16,512]{1,0:T(8,128)S(1)} %convolution_bitcast_fusion.permuted.level_three, f32[8,16]{1,0:T(8,128)S(1)} %bitcast.21, f32[8,128]{1,0:T(8,128)S(1)} %get-tuple-element.21.two, f32[8,2304]{1,0:T(8,128)S(1)} %reshape.17.basis, f32[2304,128]{1,0:T(8,128)S(1)} %bitcast.16), custom_call_target="tpu_custom_call" | custom-call | tf_op jit(solution)/shard_map/correct/pallas_call | solution.py:383
  (1 shorter events, 0.0 us)
Async XLA Ops:
  0.0 31.0 %copy-start = (f32[16,512]{1,0:T(8,128)S(1)}, f32[16,512]{1,0:T(8,128)}, u32[]{:S(2)}) copy-start(f32[16,512]{1,0:T(8,128)} %param.16) | copy-start | bytes 98308
  0.0 30.9 %copy-start.4 = (f32[8,48,48]{2,1,0:T(8,128)S(1)}, f32[8,48,48]{2,1,0:T(8,128)}, u32[]{:S(2)}) copy-start(f32[8,48,48]{2,1,0:T(8,128)} %param.12) | copy-start | bytes 221188
  0.0 31.0 %copy-start.5 = (s32[512]{0:T(512)S(1)}, s32[512]{0:T(512)}, u32[]{:S(2)}) copy-start(s32[512]{0:T(512)} %param.17) | copy-start | bytes 6148
  0.0 31.6 %copy-start.1 = (f32[1,8,16]{2,1,0:T(8,128)S(1)}, f32[1,8,16]{2,1,0:T(8,128)}, u32[]{:S(2)}) copy-start(f32[1,8,16]{2,1,0:T(8,128)} %param.15) | copy-start | bytes 1540
  0.0 31.9 %copy-start.3 = (s32[1,1,8]{2,1,0:T(1,128)S(1)}, s32[1,1,8]{2,1,0:T(1,128)}, u32[]{:S(2)}) copy-start(s32[1,1,8]{2,1,0:T(1,128)} %param.13) | copy-start | bytes 100
  5.3 27.8 %collective-permute-start = (f32[48,128]{1,0:T(8,128)S(1)}, f32[48,128]{1,0:T(8,128)S(1)}, u32[]{:S(2)}, u32[]{:S(2)}) collective-permute-start(f32[48,128]{1,0:T(8,128)S(1)} %get-tuple-element.16), channel_id=1, source_target_pairs={{32,64},{96,128},{160,192},{224,256},{288,320},{352,384},{416,448}... | collective-permute-start | bytes 73736 | tf_op jit(solution)/shard_map/ppermute | solution.py:329
  20.9 12.2 %collective-permute-start.1 = (f32[48,128]{1,0:T(8,128)S(1)}, f32[48,128]{1,0:T(8,128)S(1)}, u32[]{:S(2)}, u32[]{:S(2)}) collective-permute-start(f32[48,128]{1,0:T(8,128)S(1)} %get-tuple-element.17), channel_id=1, source_target_pairs={{1,2},{3,4},{5,6},{7,8},{9,10},{11,12},{13,14},{15,16},{17,18},{19... | collective-permute-start | bytes 73736 | tf_op jit(solution)/shard_map/ppermute | solution.py:329
  21.6 11.5 %collective-permute-start.2 = (f32[48,128]{1,0:T(8,128)S(1)}, f32[48,128]{1,0:T(8,128)S(1)}, u32[]{:S(2)}, u32[]{:S(2)}) collective-permute-start(f32[48,128]{1,0:T(8,128)S(1)} %get-tuple-element.18), channel_id=1, source_target_pairs={{0,32},{64,96},{128,160},{192,224},{256,288},{320,352},{384,416},{... | collective-permute-start | bytes 73736 | tf_op jit(solution)/shard_map/ppermute | solution.py:329
  23.5 9.6 %collective-permute-start.3 = (f32[48,128]{1,0:T(8,128)S(1)}, f32[48,128]{1,0:T(8,128)S(1)}, u32[]{:S(2)}, u32[]{:S(2)}) collective-permute-start(f32[48,128]{1,0:T(8,128)S(1)} %get-tuple-element.19), channel_id=1, source_target_pairs={{0,1},{2,3},{4,5},{6,7},{8,9},{10,11},{12,13},{14,15},{16,17},{18,... | collective-permute-start | bytes 73736 | tf_op jit(solution)/shard_map/ppermute | solution.py:329
  31.7 22.6 %copy-start.2 = (f32[1,8,256]{2,1,0:T(8,128)S(1)}, f32[1,8,256]{2,1,0:T(8,128)}, u32[]{:S(2)}) copy-start(f32[1,8,256]{2,1,0:T(8,128)} %param.14) | copy-start | bytes 24580

commit v5 on v4

--- a/solution.py
+++ b/solution.py
@@ -33,18 +33,24 @@
     return lax.dot_general(a, b, (dims, ((), ())), precision=highest, preferred_element_type=f32)
 
 
+def neighbours(source, coef_row, i, before, here_row):
+    m = coef_row.shape[0]
+    after = source[i + 2, 8 : 8 + m]
+    beside = (before + after) + (source[i + 1, 7 : 7 + m] + source[i + 1, 9 : 9 + m])
+    return after, coef_row * (beside - (4.0 + shift_mass) * here_row)
+
+
 def solve_kernel(
     kappa_hbm,
     labels,
     residual,
-    first,
-    slack,
+    zs,
+    rhs_out,
     row_far,
     col_far,
     row_near,
     col_near,
-    root_out,
-    zs,
+    kap_out,
     wide,
     rhs,
     coef,
@@ -84,19 +90,16 @@
     kap = jnp.full(here.shape, kappa[0], f32)
     for region in range(1, kappa.shape[0]):
         kap = jnp.where(here == region, kappa[region], kap)
-    root_out[...] = jnp.sqrt(kap)
+    kap_out[...] = kap
     kap_t = kap.T
     for i in range(n):
         if i % rows == 0:
             loads[i // rows].wait()
         spread = jnp.broadcast_to(kap_t[:, i : i + 1], (m, lanes))
         coef[i] = spread
-        rhs[i + 1, 8 : 8 + m] = (spread * lax.rsqrt(spread)) * loaded[i]
-
-    def neighbours(source, i, before, here_row):
-        after = source[i + 2, 8 : 8 + m]
-        beside = (before + after) + (source[i + 1, 7 : 7 + m] + source[i + 1, 9 : 9 + m])
-        return after, coef[i] * (beside - (4.0 + shift_mass) * here_row)
+        scaled = (spread * lax.rsqrt(spread)) * loaded[i]
+        rhs[i + 1, 8 : 8 + m] = scaled
+        rhs_out[i] = scaled
 
     unroll = 4
     for sweep, (keep, add) in enumerate(factors):
@@ -106,12 +109,12 @@
             for step in range(unroll):
                 i = block * unroll + step
                 if sweep == 0:
-                    after, product = neighbours(rhs, i, before, here_row)
+                    after, product = neighbours(rhs, coef[i], i, before, here_row)
                     moved = (keep * scale + add) * here_row + (add * scale) * product
                     zs[i + 1, 8 : 8 + m] = scale * here_row + moved
                 else:
-                    after, product = neighbours(zs, i, before, here_row)
-                    moved = keep * wide[i] + add * (rhs[i + 1, 8 : 8 + m] + product)
+                    after, product = neighbours(zs, coef[i], i, before, here_row)
+                    moved = keep * wide[i] + add * (rhs_out[i] + product)
                     zs[i + 1, 8 : 8 + m] = here_row + moved
                 wide[i] = moved
                 before, here_row = here_row, after
@@ -120,20 +123,14 @@
         source = rhs if sweep == 0 else zs
         lax.fori_loop(0, n // unroll, some_rows, (jnp.zeros((m, lanes), f32), source[1, 8 : 8 + m]))
 
-    before, here_row = jnp.zeros((m, lanes), f32), zs[1, 8 : 8 + m]
     even_x = lax.rem(lax.axis_index("sx"), 2) == 0
     even_y = lax.rem(lax.axis_index("sy"), 2) == 0
-    row_last = zs[n, 8 : 8 + m]
-    row_far[...] = jnp.where(even_x, here_row, row_last)
-    row_near[...] = jnp.where(even_x, row_last, here_row)
+    row_first, row_last = zs[1, 8 : 8 + m], zs[n, 8 : 8 + m]
+    row_far[...] = jnp.where(even_x, row_first, row_last)
+    row_near[...] = jnp.where(even_x, row_last, row_first)
     for i in range(n):
-        after, product = neighbours(zs, i, before, here_row)
-        inv = lax.rsqrt(coef[i])
-        slack[i] = (rhs[i + 1, 8 : 8 + m] + product) * inv
-        first[i] = here_row * inv
-        col_far[i : i + 1] = here_row[0:1]
-        col_near[i : i + 1] = here_row[m - 1 : m]
-        before, here_row = here_row, after
+        col_far[i : i + 1] = zs[i + 1, 8:9]
+        col_near[i : i + 1] = zs[i + 1, 7 + m : 8 + m]
     col_first, col_last = col_far[...], col_near[...]
     col_far[...] = jnp.where(even_y, col_first, col_last)
     col_near[...] = jnp.where(even_y, col_last, col_first)
@@ -142,12 +139,13 @@
 def solve(residual, labels, region_kappa):
     n, m, lanes = residual.shape
     field = jax.ShapeDtypeStruct((n, m, lanes), f32)
+    framed = jax.ShapeDtypeStruct((n + 2, m + 16, lanes), f32)
     edge_x = jax.ShapeDtypeStruct((m, lanes), f32)
     edge_y = jax.ShapeDtypeStruct((n, lanes), f32)
     whole = pl.BlockSpec(memory_space=pltpu.VMEM)
     return pl.pallas_call(
         solve_kernel,
-        out_shape=(field, field, edge_x, edge_y, edge_x, edge_y, jax.ShapeDtypeStruct((n, m), f32)),
+        out_shape=(framed, field, edge_x, edge_y, edge_x, edge_y, jax.ShapeDtypeStruct((n, m), f32)),
         in_specs=[
             pl.BlockSpec(memory_space=pltpu.HBM),
             pl.BlockSpec(memory_space=pltpu.HBM),
@@ -155,7 +153,6 @@
         ],
         out_specs=[whole] * 7,
         scratch_shapes=[
-            pltpu.VMEM((n + 2, m + 16, lanes), f32),
             pltpu.VMEM((n, m, lanes), f32),
             pltpu.VMEM((n + 2, m + 16, lanes), f32),
             pltpu.VMEM((n, m, lanes), f32),
@@ -184,54 +181,62 @@
     return cells
 
 
-def inner_kernel(primal, basis, slack, out):
+def inner_kernel(
+    primal, zs, rhs, basis, fields, kap, out, edge_weights, first, left, slack
+):
+    n, m, lanes = rhs.shape
+    kap_t = kap[...].T
+    before, here_row = jnp.zeros((m, lanes), f32), zs[1, 8 : 8 + m]
+    for i in range(n):
+        spread = jnp.broadcast_to(kap_t[:, i : i + 1], (m, lanes))
+        after, product = neighbours(zs, spread, i, before, here_row)
+        inv = lax.rsqrt(spread)
+        slack[i * m : (i + 1) * m] = (rhs[i] + product) * inv
+        first[i * m : (i + 1) * m] = here_row * inv
+        before, here_row = here_row, after
     cell = lax.broadcasted_iota(jnp.int32, basis.shape, 1)
     weights = basis[...] + jnp.where(cell == chosen_cells(primal, basis.shape[1]), 1.0, 0.0)
     out[...] = dot(weights, slack[...])
 
+    here = jnp.sqrt(kap[...])
+    turned = here.T
+    last = (n - 1) * m
+
+    def share(weights, begin, stride, scale):
+        cell = begin + stride * lax.broadcasted_iota(jnp.int32, weights.shape, 1)
+        chosen = jnp.where(cell == chosen_cells(primal, weights.shape[1]), 1.0, 0.0)
+        return (weights + chosen) * scale
+
+    sides = [fields[k].T for k in range(fields.shape[0])]
+    basis_first = jnp.concatenate([side[0:1] for side in sides], axis=0)
+    basis_last = jnp.concatenate([side[m - 1 : m] for side in sides], axis=0)
+    edge_weights[...] = jnp.concatenate(
+        [
+            share(basis[:, 0:m], 0, 1, here[0:1]),
+            share(basis[:, last:], last, 1, here[n - 1 :]),
+            share(basis_first, 0, m, turned[0:1]),
+            share(basis_last, m - 1, m, turned[m - 1 :]),
+        ],
+        axis=1,
+    )
+    cells = 3 * 128
+    for begin in range(0, n * m, cells):
+        b0, b1, b2 = split(basis[:, begin : begin + cells])
+        stacked = jnp.concatenate([b0, b0, b0, b1, b1, b2], axis=0)
+        left[begin : begin + cells] = stacked.T.astype(jnp.bfloat16)
+
 
 def restrict_kernel(
-    primal,
-    partial,
-    basis,
-    basis_first,
-    basis_last,
-    root,
-    row_far,
-    col_far,
-    row_near,
-    col_near,
-    restrict,
-    permuted,
-    out,
+    partial, edge_weights, row_far, col_far, row_near, col_near, restrict, permuted, out
 ):
-    n, m = root.shape
     even_x = lax.rem(lax.axis_index("sx"), 2) == 0
     even_y = lax.rem(lax.axis_index("sy"), 2) == 0
     row_low = jnp.where(even_x, row_far[...], row_near[...])
     row_high = jnp.where(even_x, row_near[...], row_far[...])
     col_low = jnp.where(even_y, col_far[...], col_near[...])
     col_high = jnp.where(even_y, col_near[...], col_far[...])
-    here = root[...]
-    turned = here.T
-    last = (n - 1) * m
-
-    def share(weights, begin, stride, scale):
-        cell = begin + stride * lax.broadcasted_iota(jnp.int32, weights.shape, 1)
-        chosen = jnp.where(cell == chosen_cells(primal, weights.shape[1]), 1.0, 0.0)
-        return (weights + chosen) * scale
-
-    weights = jnp.concatenate(
-        [
-            share(basis[:, 0:m], 0, 1, here[0:1]),
-            share(basis[:, last:], last, 1, here[n - 1 :]),
-            share(basis_first[...], 0, m, turned[0:1]),
-            share(basis_last[...], m - 1, m, turned[m - 1 :]),
-        ],
-        axis=1,
-    )
     halo = jnp.concatenate([row_low, row_high, col_low, col_high], axis=0)
-    both = jnp.concatenate([partial[...] + dot(weights, halo), restrict[...]], axis=0)
+    both = jnp.concatenate([partial[...] + dot(edge_weights[...], halo), restrict[...]], axis=0)
     height = both.shape[0]
     for member in range(out.shape[0] // height):
         out[member * height : (member + 1) * height] = both
@@ -268,7 +273,7 @@
     return high, mid, rest - mid
 
 
-def correct_kernel(terms, level_three, restrict, two, basis, first, result, held, sem):
+def correct_kernel(terms, level_three, restrict, two, left, first, result, held, sem):
     members, height, lanes = terms.shape
     placed = jnp.concatenate([terms[member] for member in range(members)], axis=0)
     three = dot(level_three[...], placed)
@@ -280,9 +285,7 @@
     copies = []
     for piece in range(pieces):
         at = pl.ds(piece * cells, cells)
-        b0, b1, b2 = split(basis[:, piece * cells : (piece + 1) * cells])
-        left = jnp.concatenate([b0, b0, b0, b1, b1, b2], axis=0).T.astype(jnp.bfloat16)
-        held[at] = first[at] + jnp.dot(left, right, preferred_element_type=f32)
+        held[at] = first[at] + jnp.dot(left[at], right, preferred_element_type=f32)
         copy = pltpu.make_async_copy(held.at[at], result.at[at], sem.at[piece])
         copy.start()
         copies.append(copy)
@@ -290,13 +293,14 @@
         copy.wait()
 
 
-def vmem_call(body, out_shape, inputs, name, scalars=0):
+def vmem_call(body, out_shape, inputs, name, scalars=0, scratch=()):
     whole = pl.BlockSpec(memory_space=pltpu.VMEM)
     return pl.pallas_call(
         body,
         out_shape=out_shape,
         in_specs=[pl.BlockSpec(memory_space=pltpu.SMEM)] * scalars + [whole] * (len(inputs) - scalars),
         out_specs=jax.tree.map(lambda _: whole, out_shape),
+        scratch_shapes=scratch,
         compiler_params=pltpu.CompilerParams(vmem_limit_bytes=VMEM_LIMIT),
         name=name,
     )(*inputs)
@@ -321,7 +325,7 @@
     coarse_third = local_restrict.shape[1]
     members_x, members_y = lax.axis_size("sx"), lax.axis_size("sy")
 
-    first, slack, row_far, col_far, row_near, col_near, root = solve(residual, labels, region_kappa)
+    zs, rhs, row_far, col_far, row_near, col_near, kap = solve(residual, labels, region_kappa)
 
     def swapped(edge, axis, begin):
         count = lax.axis_size(axis)
@@ -335,12 +339,18 @@
 
     primal = primal_cells.reshape(-1)
     basis_cells = coarse_basis.reshape(coarse_count, cell_count)
-    partial = vmem_call(
+    partial, edge_weights, first, left = vmem_call(
         inner_kernel,
-        jax.ShapeDtypeStruct((coarse_count, rhs_count), f32),
-        (primal, basis_cells, slack.reshape(cell_count, rhs_count)),
+        (
+            jax.ShapeDtypeStruct((coarse_count, rhs_count), f32),
+            jax.ShapeDtypeStruct((coarse_count, 2 * (cells_x + cells_y)), f32),
+            jax.ShapeDtypeStruct((cell_count, rhs_count), f32),
+            jax.ShapeDtypeStruct((cell_count, 6 * coarse_count), jnp.bfloat16),
+        ),
+        (primal, zs, rhs, basis_cells, coarse_basis, kap),
         "inner",
         scalars=1,
+        scratch=(pltpu.VMEM((cell_count, rhs_count), f32),),
     )
     order_table = (
         row_order[None, :] == jnp.arange(row_order.shape[0], dtype=jnp.int32)[:, None]
@@ -351,12 +361,8 @@
         restrict_kernel,
         jax.ShapeDtypeStruct((members_y * (coarse_count + 1), rhs_count), f32),
         (
-            primal,
             partial,
-            basis_cells,
-            coarse_basis[:, :, 0],
-            coarse_basis[:, :, -1],
-            root,
+            edge_weights,
             row_far,
             col_far,
             row_near,
@@ -365,7 +371,6 @@
             permuted,
         ),
         "restrict",
-        scalars=1,
     )
     everyone = lax.all_to_all(copies[:, None], "sy", 0, 0, tiled=True)[:, 0]
     two, copies = vmem_call(
@@ -388,7 +393,7 @@
         scratch_shapes=[pltpu.VMEM((cell_count, rhs_count), f32), pltpu.SemaphoreType.DMA((6,))],
         compiler_params=pltpu.CompilerParams(vmem_limit_bytes=VMEM_LIMIT),
         name="correct",
-    )(terms, permuted, local_restrict, two, basis_cells, first.reshape(cell_count, rhs_count))
+    )(terms, permuted, local_restrict, two, left, first)
     return result.reshape(cells_x, cells_y, rhs_count)
 
 

time: 80.9 us -> 80.1 us (level)
  transfers between devices with their start and end apart: 4 -> 4, of which waited for: 0 -> 0; matrix products, arithmetic and copies ran while one was open for 1% -> 1% of each run, Pallas kernels for 1% -> 2%
where the time goes in v5:
time: 80.1 us; the launch traced here: 79.8 us
  blocking collectives  44.6 us (56%)
  starting transfers between devices  25.6 us (32%)
  Pallas kernels  8.82 us (11%)
    ppermute x4, starting transfers between devices, swapped(): lax.ppermute(edge, axis, pairs + [(target, source) for source, target in...  25.6 us
    all_to_all x1, blocking collectives, shards(): terms = lax.all_to_all(copies, 'sx', 0, 0, tiled=True)  24.4 us
    all_to_all x1, blocking collectives, shards(): everyone = lax.all_to_all(copies[:, None], 'sy', 0, 0, tiled=True)[:, 0]  20.3 us
    pallas_call x1, Pallas kernels, solve(): pl.pallas_call(solve_kernel, out_shape=(framed, field, edge_x, edge_y, ed...  4.89 us
    pallas_call x3, Pallas kernels, vmem_call(): pl.pallas_call(body, out_shape=out_shape, in_specs=[pl.BlockSpec(memory_s...  2.33 us
    pallas_call x1, Pallas kernels, shards(): pl.pallas_call(correct_kernel, out_shape=jax.ShapeDtypeStruct((cell_count...  1.6 us
  transfers between devices with their start and end apart: 4, of which 0 were waited for; matrix products, arithmetic and copies ran while one was open for 1% of the time, Pallas kernels for 2%

profile of v5, /device:TPU:1, one launch (start us, length us, event | category | flops | bytes accessed | tf_op | source)
XLA Modules:
  0.0 79.8 jit_solution(3864607034314876448)
XLA Ops:
  0.0 0.0 copy-start
  0.0 0.0 copy-start.5
  0.0 0.0 copy-start.1
  0.0 0.0 copy-start.2
  0.0 0.0 copy-start.4
  0.0 4.9 %solve.1 = (f32[50,64,128]{2,1,0:T(8,128)S(1)}, f32[48,48,128]{2,1,0:T(8,128)S(1)}, f32[48,128]{1,0:T(8,128)S(1)}, f32[48,128]{1,0:T(8,128)S(1)}, f32[48,128]{1,...) custom-call(f32[8]{0:T(128)} %kappa_hbm.1, s32[48,48]{1,0:T(8,128)} %labels.1, f32[48,48,128]{2,1,0:T(8,128)} %residual.1), custom_call_target="tpu_custom_call" | custom-call | flops 23592960 | bytes 3538944 | tf_op jit(solution)/shard_map/solve/pallas_call | solution.py:146
  4.9 15.7 %collective-permute-start = (f32[48,128]{1,0:T(8,128)S(1)}, f32[48,128]{1,0:T(8,128)S(1)}, u32[]{:S(2)}, u32[]{:S(2)}) collective-permute-start(f32[48,128]{1,0:T(8,128)S(1)} %get-tuple-element.23), channel_id=1, source_target_pairs={{32,64},{96,128},{160,192},{224,256},{288,320},{352,384},{416,448}... | collective-permute-start | bytes 73736 | tf_op jit(solution)/shard_map/ppermute | solution.py:333
  20.6 0.7 collective-permute-start.1
  21.3 1.9 %collective-permute-start.2 = (f32[48,128]{1,0:T(8,128)S(1)}, f32[48,128]{1,0:T(8,128)S(1)}, u32[]{:S(2)}, u32[]{:S(2)}) collective-permute-start(f32[48,128]{1,0:T(8,128)S(1)} %get-tuple-element.25), channel_id=1, source_target_pairs={{0,32},{64,96},{128,160},{192,224},{256,288},{320,352},{384,416},{... | collective-permute-start | bytes 73736 | tf_op jit(solution)/shard_map/ppermute | solution.py:333
  23.2 7.4 %collective-permute-start.3 = (f32[48,128]{1,0:T(8,128)S(1)}, f32[48,128]{1,0:T(8,128)S(1)}, u32[]{:S(2)}, u32[]{:S(2)}) collective-permute-start(f32[48,128]{1,0:T(8,128)S(1)} %get-tuple-element.26), channel_id=1, source_target_pairs={{0,1},{2,3},{4,5},{6,7},{8,9},{10,11},{12,13},{14,15},{16,17},{18,... | collective-permute-start | bytes 73736 | tf_op jit(solution)/shard_map/ppermute | solution.py:333
  30.6 0.0 copy-done
  30.6 0.0 copy-done.5
  30.6 0.4 convolution_bitcast_fusion.permuted.level_three
  31.0 0.0 copy-done.1
  31.0 0.1 reshape.11.basis
  31.1 0.0 copy-done.2
  31.1 0.1 reshape_squeeze.3.restrict
  31.2 0.0 copy-done.4
  31.2 0.0 copy-start.3
  31.2 1.8 %inner.1 = (f32[8,128]{1,0:T(8,128)S(1)}, f32[8,192]{1,0:T(8,128)S(1)}, f32[2304,128]{1,0:T(8,128)S(1)}, bf16[2304,48]{1,0:T(8,128)(2,1)S(1)}) custom-call(s32[8]{0:T(128)S(1)} %bitcast.15, f32[50,64,128]{2,1,0:T(8,128)S(1)} %get-tuple-element.18.zs, f32[48,48,128]{2,1,0:T(8,128)S(1)} %get-tuple-element.19.rhs, f32[8,2304]{1,0:T(8,128)S(1)} %reshape.11.basis, ...), custom_call_target="tpu_custom_call" | custom-call | tf_op jit(solution)/shard_map/inner/pallas_call | solution.py:298
  33.0 0.0 collective-permute-done.row_far
  33.0 0.0 collective-permute-done.1.col_far
  33.0 0.0 collective-permute-done.2.row_near
  33.0 0.0 collective-permute-done.3.col_near
  33.0 0.2 restrict.1
  33.3 20.3 %all_to_all.10 = f32[288,1,128]{2,1,0:T(1,128)S(1)} all-to-all(f32[288,1,128]{2,1,0:T(1,128)S(1)} %bitcast.11), channel_id=1, replica_groups=mesh['sx'=32,'sy'=32] {'sy'}, dimensions={0} | all-to-all | bytes 294912 | tf_op jit(solution)/shard_map/all_to_all | solution.py:375
  53.5 0.0 copy-done.3
  53.5 0.3 row.1
  53.9 24.4 %all_to_all.11.terms = f32[32,16,128]{2,1,0:T(8,128)S(1)} all-to-all(f32[32,16,128]{2,1,0:T(8,128)S(1)} %get-tuple-element.27), channel_id=1, replica_groups=mesh['sx'=32,'sy'=32] {'sx'}, dimensions={0} | all-to-all | bytes 524288 | tf_op jit(solution)/shard_map/all_to_all | solution.py:385
  78.2 1.6 %correct.1 = f32[2304,128]{1,0:T(8,128)} custom-call(f32[32,16,128]{2,1,0:T(8,128)S(1)} %all_to_all.11.terms, f32[16,512]{1,0:T(8,128)S(1)} %convolution_bitcast_fusion.permuted.level_three, f32[8,16]{1,0:T(8,128)S(1)} %bitcast.13, f32[8,128]{1,0:T(8,128)S(1)} %get-tuple-element.28.two, bf16[2304,48]{1,0:T(8,128)(2,1)S(1)} %get-tuple-element.29.left, ...), custom_call_target="tpu_custom_call" | custom-call | tf_op jit(solution)/shard_map/correct/pallas_call | solution.py:388
Async XLA Ops:
  0.0 30.6 %copy-start = (f32[16,512]{1,0:T(8,128)S(1)}, f32[16,512]{1,0:T(8,128)}, u32[]{:S(2)}) copy-start(f32[16,512]{1,0:T(8,128)} %param.16) | copy-start | bytes 98308
  0.0 30.6 %copy-start.5 = (s32[512]{0:T(512)S(1)}, s32[512]{0:T(512)}, u32[]{:S(2)}) copy-start(s32[512]{0:T(512)} %param.17) | copy-start | bytes 6148
  0.0 31.0 %copy-start.1 = (f32[8,48,48]{2,1,0:T(8,128)S(1)}, f32[8,48,48]{2,1,0:T(8,128)}, u32[]{:S(2)}) copy-start(f32[8,48,48]{2,1,0:T(8,128)} %fields.1) | copy-start | bytes 221188
  0.0 31.1 %copy-start.2 = (f32[1,8,16]{2,1,0:T(8,128)S(1)}, f32[1,8,16]{2,1,0:T(8,128)}, u32[]{:S(2)}) copy-start(f32[1,8,16]{2,1,0:T(8,128)} %param.15) | copy-start | bytes 1540
  0.0 31.2 %copy-start.4 = (s32[1,1,8]{2,1,0:T(1,128)S(1)}, s32[1,1,8]{2,1,0:T(1,128)}, u32[]{:S(2)}) copy-start(s32[1,1,8]{2,1,0:T(1,128)} %param.13) | copy-start | bytes 100
  4.9 28.1 %collective-permute-start = (f32[48,128]{1,0:T(8,128)S(1)}, f32[48,128]{1,0:T(8,128)S(1)}, u32[]{:S(2)}, u32[]{:S(2)}) collective-permute-start(f32[48,128]{1,0:T(8,128)S(1)} %get-tuple-element.23), channel_id=1, source_target_pairs={{32,64},{96,128},{160,192},{224,256},{288,320},{352,384},{416,448}... | collective-permute-start | bytes 73736 | tf_op jit(solution)/shard_map/ppermute | solution.py:333
  20.6 12.4 %collective-permute-start.1 = (f32[48,128]{1,0:T(8,128)S(1)}, f32[48,128]{1,0:T(8,128)S(1)}, u32[]{:S(2)}, u32[]{:S(2)}) collective-permute-start(f32[48,128]{1,0:T(8,128)S(1)} %get-tuple-element.24), channel_id=1, source_target_pairs={{1,2},{3,4},{5,6},{7,8},{9,10},{11,12},{13,14},{15,16},{17,18},{19... | collective-permute-start | bytes 73736 | tf_op jit(solution)/shard_map/ppermute | solution.py:333
  21.3 11.8 %collective-permute-start.2 = (f32[48,128]{1,0:T(8,128)S(1)}, f32[48,128]{1,0:T(8,128)S(1)}, u32[]{:S(2)}, u32[]{:S(2)}) collective-permute-start(f32[48,128]{1,0:T(8,128)S(1)} %get-tuple-element.25), channel_id=1, source_target_pairs={{0,32},{64,96},{128,160},{192,224},{256,288},{320,352},{384,416},{... | collective-permute-start | bytes 73736 | tf_op jit(solution)/shard_map/ppermute | solution.py:333
  23.2 9.8 %collective-permute-start.3 = (f32[48,128]{1,0:T(8,128)S(1)}, f32[48,128]{1,0:T(8,128)S(1)}, u32[]{:S(2)}, u32[]{:S(2)}) collective-permute-start(f32[48,128]{1,0:T(8,128)S(1)} %get-tuple-element.26), channel_id=1, source_target_pairs={{0,1},{2,3},{4,5},{6,7},{8,9},{10,11},{12,13},{14,15},{16,17},{18,... | collective-permute-start | bytes 73736 | tf_op jit(solution)/shard_map/ppermute | solution.py:333
  31.2 22.3 %copy-start.3 = (f32[1,8,256]{2,1,0:T(8,128)S(1)}, f32[1,8,256]{2,1,0:T(8,128)}, u32[]{:S(2)}) copy-start(f32[1,8,256]{2,1,0:T(8,128)} %param.14) | copy-start | bytes 24580

commit v6 on v5

--- a/solution.py
+++ b/solution.py
@@ -48,8 +48,8 @@
     rhs_out,
     row_far,
     col_far,
+    col_near,
     row_near,
-    col_near,
     kap_out,
     wide,
     rhs,
@@ -145,7 +145,7 @@
     whole = pl.BlockSpec(memory_space=pltpu.VMEM)
     return pl.pallas_call(
         solve_kernel,
-        out_shape=(framed, field, edge_x, edge_y, edge_x, edge_y, jax.ShapeDtypeStruct((n, m), f32)),
+        out_shape=(framed, field, edge_x, edge_y, edge_y, edge_x, jax.ShapeDtypeStruct((n, m), f32)),
         in_specs=[
             pl.BlockSpec(memory_space=pltpu.HBM),
             pl.BlockSpec(memory_space=pltpu.HBM),
@@ -227,7 +227,7 @@
 
 
 def restrict_kernel(
-    partial, edge_weights, row_far, col_far, row_near, col_near, restrict, permuted, out
+    partial, edge_weights, row_far, col_far, col_near, row_near, restrict, permuted, out
 ):
     even_x = lax.rem(lax.axis_index("sx"), 2) == 0
     even_y = lax.rem(lax.axis_index("sy"), 2) == 0
@@ -325,7 +325,7 @@
     coarse_third = local_restrict.shape[1]
     members_x, members_y = lax.axis_size("sx"), lax.axis_size("sy")
 
-    zs, rhs, row_far, col_far, row_near, col_near, kap = solve(residual, labels, region_kappa)
+    zs, rhs, row_far, col_far, col_near, row_near, kap = solve(residual, labels, region_kappa)
 
     def swapped(edge, axis, begin):
         count = lax.axis_size(axis)
@@ -334,8 +334,8 @@
 
     row_far = swapped(row_far, "sx", 1)
     col_far = swapped(col_far, "sy", 1)
+    col_near = swapped(col_near, "sy", 0)
     row_near = swapped(row_near, "sx", 0)
-    col_near = swapped(col_near, "sy", 0)
 
     primal = primal_cells.reshape(-1)
     basis_cells = coarse_basis.reshape(coarse_count, cell_count)
@@ -365,8 +365,8 @@
             edge_weights,
             row_far,
             col_far,
+            col_near,
             row_near,
-            col_near,
             local_restrict.reshape(1, coarse_count * coarse_third),
             permuted,
         ),

time: 80.1 us -> 80.4 us (level)
  no operation moved by 1% of the time
where the time goes in v6:
time: 80.4 us; the launch traced here: 80.1 us
  blocking collectives  44.9 us (56%)
  starting transfers between devices  25.6 us (32%)
  Pallas kernels  8.82 us (11%)
    ppermute x4, starting transfers between devices, swapped(): lax.ppermute(edge, axis, pairs + [(target, source) for source, target in...  25.6 us
    all_to_all x1, blocking collectives, shards(): terms = lax.all_to_all(copies, 'sx', 0, 0, tiled=True)  24.7 us
    all_to_all x1, blocking collectives, shards(): everyone = lax.all_to_all(copies[:, None], 'sy', 0, 0, tiled=True)[:, 0]  20.2 us
    pallas_call x1, Pallas kernels, solve(): pl.pallas_call(solve_kernel, out_shape=(framed, field, edge_x, edge_y, ed...  4.89 us
    pallas_call x3, Pallas kernels, vmem_call(): pl.pallas_call(body, out_shape=out_shape, in_specs=[pl.BlockSpec(memory_s...  2.33 us
  transfers between devices with their start and end apart: 4, of which 0 were waited for; matrix products, arithmetic and copies ran while one was open for 1% of the time, Pallas kernels for 2%

profile of v6, /device:TPU:1, one launch (start us, length us, event | category | flops | bytes accessed | tf_op | source)
XLA Modules:
  0.0 80.1 jit_solution(10393446408408340220)
XLA Ops:
  0.0 0.0 copy-start
  0.0 0.0 copy-start.5
  0.0 0.0 copy-start.1
  0.0 0.0 copy-start.2
  0.0 0.0 copy-start.4
  0.0 4.9 %solve.1 = (f32[50,64,128]{2,1,0:T(8,128)S(1)}, f32[48,48,128]{2,1,0:T(8,128)S(1)}, f32[48,128]{1,0:T(8,128)S(1)}, f32[48,128]{1,0:T(8,128)S(1)}, f32[48,128]{1,...) custom-call(f32[8]{0:T(128)} %kappa_hbm.1, s32[48,48]{1,0:T(8,128)} %labels.1, f32[48,48,128]{2,1,0:T(8,128)} %residual.1), custom_call_target="tpu_custom_call" | custom-call | flops 23592960 | bytes 3538944 | tf_op jit(solution)/shard_map/solve/pallas_call | solution.py:146
  4.9 15.7 %collective-permute-start = (f32[48,128]{1,0:T(8,128)S(1)}, f32[48,128]{1,0:T(8,128)S(1)}, u32[]{:S(2)}, u32[]{:S(2)}) collective-permute-start(f32[48,128]{1,0:T(8,128)S(1)} %get-tuple-element.23), channel_id=1, source_target_pairs={{32,64},{96,128},{160,192},{224,256},{288,320},{352,384},{416,448}... | collective-permute-start | bytes 73736 | tf_op jit(solution)/shard_map/ppermute | solution.py:333
  20.6 0.7 collective-permute-start.1
  21.3 7.4 %collective-permute-start.2 = (f32[48,128]{1,0:T(8,128)S(1)}, f32[48,128]{1,0:T(8,128)S(1)}, u32[]{:S(2)}, u32[]{:S(2)}) collective-permute-start(f32[48,128]{1,0:T(8,128)S(1)} %get-tuple-element.25), channel_id=1, source_target_pairs={{0,1},{2,3},{4,5},{6,7},{8,9},{10,11},{12,13},{14,15},{16,17},{18,... | collective-permute-start | bytes 73736 | tf_op jit(solution)/shard_map/ppermute | solution.py:333
  28.6 1.9 %collective-permute-start.3 = (f32[48,128]{1,0:T(8,128)S(1)}, f32[48,128]{1,0:T(8,128)S(1)}, u32[]{:S(2)}, u32[]{:S(2)}) collective-permute-start(f32[48,128]{1,0:T(8,128)S(1)} %get-tuple-element.26), channel_id=1, source_target_pairs={{0,32},{64,96},{128,160},{192,224},{256,288},{320,352},{384,416},{... | collective-permute-start | bytes 73736 | tf_op jit(solution)/shard_map/ppermute | solution.py:333
  30.6 0.0 copy-done
  30.6 0.0 copy-done.5
  30.6 0.4 convolution_bitcast_fusion.permuted.level_three
  31.0 0.0 copy-done.1
  31.0 0.1 reshape.11.basis
  31.1 0.0 copy-done.2
  31.1 0.1 reshape_squeeze.3.restrict
  31.2 0.0 copy-done.4
  31.2 0.0 copy-start.3
  31.2 1.8 %inner.1 = (f32[8,128]{1,0:T(8,128)S(1)}, f32[8,192]{1,0:T(8,128)S(1)}, f32[2304,128]{1,0:T(8,128)S(1)}, bf16[2304,48]{1,0:T(8,128)(2,1)S(1)}) custom-call(s32[8]{0:T(128)S(1)} %bitcast.15, f32[50,64,128]{2,1,0:T(8,128)S(1)} %get-tuple-element.18.zs, f32[48,48,128]{2,1,0:T(8,128)S(1)} %get-tuple-element.19.rhs, f32[8,2304]{1,0:T(8,128)S(1)} %reshape.11.basis, ...), custom_call_target="tpu_custom_call" | custom-call | tf_op jit(solution)/shard_map/inner/pallas_call | solution.py:298
  33.0 0.0 collective-permute-done.row_far
  33.0 0.0 collective-permute-done.1.col_far
  33.0 0.0 collective-permute-done.2.col_near
  33.0 0.0 collective-permute-done.3.row_near
  33.0 0.2 restrict.1
  33.3 20.2 %all_to_all.10 = f32[288,1,128]{2,1,0:T(1,128)S(1)} all-to-all(f32[288,1,128]{2,1,0:T(1,128)S(1)} %bitcast.11), channel_id=1, replica_groups=mesh['sx'=32,'sy'=32] {'sy'}, dimensions={0} | all-to-all | bytes 294912 | tf_op jit(solution)/shard_map/all_to_all | solution.py:375
  53.5 0.0 copy-done.3
  53.5 0.3 row.1
  53.9 24.7 %all_to_all.11.terms = f32[32,16,128]{2,1,0:T(8,128)S(1)} all-to-all(f32[32,16,128]{2,1,0:T(8,128)S(1)} %get-tuple-element.27), channel_id=1, replica_groups=mesh['sx'=32,'sy'=32] {'sx'}, dimensions={0} | all-to-all | bytes 524288 | tf_op jit(solution)/shard_map/all_to_all | solution.py:385
  78.5 1.6 %correct.1 = f32[2304,128]{1,0:T(8,128)} custom-call(f32[32,16,128]{2,1,0:T(8,128)S(1)} %all_to_all.11.terms, f32[16,512]{1,0:T(8,128)S(1)} %convolution_bitcast_fusion.permuted.level_three, f32[8,16]{1,0:T(8,128)S(1)} %bitcast.13, f32[8,128]{1,0:T(8,128)S(1)} %get-tuple-element.28.two, bf16[2304,48]{1,0:T(8,128)(2,1)S(1)} %get-tuple-element.29.left, ...), custom_call_target="tpu_custom_call" | custom-call | tf_op jit(solution)/shard_map/correct/pallas_call | solution.py:388
Async XLA Ops:
  0.0 30.6 %copy-start = (f32[16,512]{1,0:T(8,128)S(1)}, f32[16,512]{1,0:T(8,128)}, u32[]{:S(2)}) copy-start(f32[16,512]{1,0:T(8,128)} %param.16) | copy-start | bytes 98308
  0.0 30.6 %copy-start.5 = (s32[512]{0:T(512)S(1)}, s32[512]{0:T(512)}, u32[]{:S(2)}) copy-start(s32[512]{0:T(512)} %param.17) | copy-start | bytes 6148
  0.0 31.0 %copy-start.1 = (f32[8,48,48]{2,1,0:T(8,128)S(1)}, f32[8,48,48]{2,1,0:T(8,128)}, u32[]{:S(2)}) copy-start(f32[8,48,48]{2,1,0:T(8,128)} %fields.1) | copy-start | bytes 221188
  0.0 31.1 %copy-start.2 = (f32[1,8,16]{2,1,0:T(8,128)S(1)}, f32[1,8,16]{2,1,0:T(8,128)}, u32[]{:S(2)}) copy-start(f32[1,8,16]{2,1,0:T(8,128)} %param.15) | copy-start | bytes 1540
  0.0 31.2 %copy-start.4 = (s32[1,1,8]{2,1,0:T(1,128)S(1)}, s32[1,1,8]{2,1,0:T(1,128)}, u32[]{:S(2)}) copy-start(s32[1,1,8]{2,1,0:T(1,128)} %param.13) | copy-start | bytes 100
  4.9 28.1 %collective-permute-start = (f32[48,128]{1,0:T(8,128)S(1)}, f32[48,128]{1,0:T(8,128)S(1)}, u32[]{:S(2)}, u32[]{:S(2)}) collective-permute-start(f32[48,128]{1,0:T(8,128)S(1)} %get-tuple-element.23), channel_id=1, source_target_pairs={{32,64},{96,128},{160,192},{224,256},{288,320},{352,384},{416,448}... | collective-permute-start | bytes 73736 | tf_op jit(solution)/shard_map/ppermute | solution.py:333
  20.6 12.4 %collective-permute-start.1 = (f32[48,128]{1,0:T(8,128)S(1)}, f32[48,128]{1,0:T(8,128)S(1)}, u32[]{:S(2)}, u32[]{:S(2)}) collective-permute-start(f32[48,128]{1,0:T(8,128)S(1)} %get-tuple-element.24), channel_id=1, source_target_pairs={{1,2},{3,4},{5,6},{7,8},{9,10},{11,12},{13,14},{15,16},{17,18},{19... | collective-permute-start | bytes 73736 | tf_op jit(solution)/shard_map/ppermute | solution.py:333
  21.3 11.8 %collective-permute-start.2 = (f32[48,128]{1,0:T(8,128)S(1)}, f32[48,128]{1,0:T(8,128)S(1)}, u32[]{:S(2)}, u32[]{:S(2)}) collective-permute-start(f32[48,128]{1,0:T(8,128)S(1)} %get-tuple-element.25), channel_id=1, source_target_pairs={{0,1},{2,3},{4,5},{6,7},{8,9},{10,11},{12,13},{14,15},{16,17},{18,... | collective-permute-start | bytes 73736 | tf_op jit(solution)/shard_map/ppermute | solution.py:333
  28.6 4.4 %collective-permute-start.3 = (f32[48,128]{1,0:T(8,128)S(1)}, f32[48,128]{1,0:T(8,128)S(1)}, u32[]{:S(2)}, u32[]{:S(2)}) collective-permute-start(f32[48,128]{1,0:T(8,128)S(1)} %get-tuple-element.26), channel_id=1, source_target_pairs={{0,32},{64,96},{128,160},{192,224},{256,288},{320,352},{384,416},{... | collective-permute-start | bytes 73736 | tf_op jit(solution)/shard_map/ppermute | solution.py:333
  31.2 22.3 %copy-start.3 = (f32[1,8,256]{2,1,0:T(8,128)S(1)}, f32[1,8,256]{2,1,0:T(8,128)}, u32[]{:S(2)}) copy-start(f32[1,8,256]{2,1,0:T(8,128)} %param.14) | copy-start | bytes 24580
